TPU v7x, 256 devices: a whole 4x4x8 slice. The times are simulated.
256 devices in a mesh: dp: 16 (over z, y_lo), dep: 4 (over x), hgt: 4 (over y_hi, core).
Axes of the slice: x: 4, y: 4 (y_hi: 2, y_lo: 2; y = y_hi * 2 + y_lo), z: 8, core: 2. Of those that a mesh axis runs over, the one named last changes fastest.
Arguments:
- volume: bfloat16 [16, 32, 8, 32, 128], P('dp', None, 'dep', 'hgt'), may hold values from -6 to 6
- kernel_first: bfloat16 [27, 64, 32], replicated, may hold values from -0.21875 to 0.21875
- kernel_second: bfloat16 [27, 128, 64], replicated, may hold values from -0.15625 to 0.15625
- cotangent: bfloat16 [16, 128, 8, 32, 128], P('dp', None, 'dep', 'hgt'), may hold values from -0.01171875 to 0.01171875
Outputs:
- features: bfloat16 [16, 128, 8, 32, 128], P('dp', None, 'dep', 'hgt')
- grad_first: float32 [27, 64, 32], P(None, 'dp')
- grad_second: float32 [27, 128, 64], P(None, 'dp')
All inputs are finite; a program needn't handle non-finite values.
Results may differ from a plain program's by a relative error of at most 0.0049.
Values may be sent and summed in bfloat16 or wider, within the bound.
A program may use at most 64 MiB of HBM per device.

v0:
```python
import jax
import jax.numpy as jnp
from jax import lax
from jax.sharding import PartitionSpec as P

OFFSETS = [
    (first, second, third) for first in (-1, 0, 1) for second in (-1, 0, 1) for third in (-1, 0, 1)
]


def extended_2(x, sides, width):
    for axis, dim in sides:
        size, length = (lax.axis_size(axis), x.shape[dim])
        up = [(i, (i + 1) % size) for i in range(size - 1)]
        down = [(j, i) for i, j in up]
        last = lax.slice_in_dim(x, length - width, length, axis=dim)
        leading = lax.slice_in_dim(x, 0, width, axis=dim)
        before = lax.ppermute(last, axis, up)
        after = lax.ppermute(leading, axis, down)
        x = jnp.concatenate([before, x, after], axis=dim)
    return x


def widen(field):
    return jnp.pad(field, ((0, 0), (0, 0), (0, 0), (0, 0), (1, 1)))


def window(padded, shift_d, shift_h, shift_w, depth, height, width):
    return padded[
        :,
        :,
        1 + shift_d : 1 + shift_d + depth,
        1 + shift_h : 1 + shift_h + height,
        1 + shift_w : 1 + shift_w + width,
    ]


def convolve(extended, kernel, depth, height, width):
    padded = widen(extended)
    total = None
    for number, shift in enumerate(OFFSETS):
        piece = window(padded, shift[0], shift[1], shift[2], depth, height, width)
        term = jnp.einsum(
            "oi,bidhw->bodhw", kernel[number], piece, preferred_element_type=jnp.float32
        )
        total = term if total is None else total + term
    return total


def kernel_grad(upstream, extended, depth, height, width):
    padded = widen(extended)
    parts = []
    for shift in OFFSETS:
        piece = window(padded, shift[0], shift[1], shift[2], depth, height, width)
        parts.append(
            jnp.einsum("bodhw,bidhw->oi", upstream, piece, preferred_element_type=jnp.float32)
        )
    return jnp.stack(parts)


def per_device(volume, kernel_first, kernel_second, cotangent):
    depth, height, width = (volume.shape[2], volume.shape[3], volume.shape[4])
    vol_rim = extended_2(volume, (("dep", 2), ("hgt", 3)), 1)
    pre = convolve(vol_rim, kernel_first, depth, height, width)
    hidden = jax.nn.silu(pre).astype(jnp.bfloat16)
    hidden_rim = extended_2(hidden, (("dep", 2), ("hgt", 3)), 1)
    features = convolve(hidden_rim, kernel_second, depth, height, width).astype(jnp.bfloat16)
    cot_rim = extended_2(cotangent, (("dep", 2), ("hgt", 3)), 1)
    grad_second = kernel_grad(cotangent, hidden_rim, depth, height, width)
    padded_cot = widen(cot_rim)
    back = None
    for number, shift in enumerate(OFFSETS):
        piece = window(padded_cot, -shift[0], -shift[1], -shift[2], depth, height, width)
        term = jnp.einsum(
            "oi,bodhw->bidhw", kernel_second[number], piece, preferred_element_type=jnp.float32
        )
        back = term if back is None else back + term
    sigma = jax.nn.sigmoid(pre)
    delta = (back * (sigma * (1.0 + pre * (1.0 - sigma)))).astype(jnp.bfloat16)
    grad_first = kernel_grad(delta, vol_rim, depth, height, width)
    summed = lax.psum((grad_first, grad_second), ("dep", "hgt"))
    grad_first, grad_second = (
        lax.psum_scatter(summed[0], "dp", scatter_dimension=1, tiled=True),
        lax.psum_scatter(summed[1], "dp", scatter_dimension=1, tiled=True),
    )
    return (features, grad_first, grad_second)


def solution(mesh):
    placed = (P("dp", None, "dep", "hgt", None), P(), P(), P("dp", None, "dep", "hgt", None))
    return jax.shard_map(
        per_device,
        mesh=mesh,
        in_specs=placed,
        out_specs=(P("dp", None, "dep", "hgt", None), P(None, "dp", None), P(None, "dp", None)),
        check_vma=False,
    )
```

profile of v0, /device:TPU:1, one launch (start us, length us, event | category | flops | bytes accessed | tf_op | source)
XLA Modules:
  0.0 417.5 jit_solution(17139515704096667886)
XLA Ops:
  7.2 0.9 copy.50
  8.2 4.1 collective-permute-start
  12.3 1.4 collective-permute-start.1
  13.7 1.2 copy.56
  14.9 4.0 collective-permute-start.8
  19.0 1.3 collective-permute-start.9
  20.4 6.2 %collective-permute-start.2 = (bf16[1,32,4,1,128]{4,1,3,2,0:T(8,128)(2,1)S(1)}, bf16[1,32,4,1,128]{4,1,3,2,0:T(8,128)(2,1)S(1)}, u32[]{:S(2)}, u32[]{:S(2)}) collective-permute-start(bf16[1,32,4,1,128]{4,1,3,2,0:T(8,128)(2,1)S(1)} %get-tuple-element.21), channel_id=1, source_target_pairs={{0,1},{1,2},{2,3},{4,5},{5,6},{6,7},{8,9},{9,10},{10,11},{12,13},{... | collective-permute-start | bytes 98312 | tf_op jit(solution)/shard_map/ppermute | solution.py:18
  26.6 1.9 collective-permute-start.3
  28.8 4.5 %collective-permute-done.3 = bf16[1,32,4,1,128]{4,1,3,2,0:T(8,128)(2,1)S(1)} collective-permute-done((bf16[1,32,4,1,128]{4,1,3,2,0:T(8,128)(2,1)S(1)}, bf16[1,32,4,1,128]{4,1,3,2,0:T(8,128)(2,1)S(1)}, u32[]{:S(2)}, u32[]{:S(2)}) %collective-permute-start.3) | collective-permute-done | bytes 32800 | tf_op jit(solution)/shard_map/ppermute | solution.py:19
  41.6 4.3 %collective-permute-start.4 = (bf16[1,64,1,8,128]{4,1,3,2,0:T(8,128)(2,1)S(1)}, bf16[1,64,1,8,128]{4,1,3,2,0:T(8,128)(2,1)S(1)}, u32[]{:S(2)}, u32[]{:S(2)}) collective-permute-start(bf16[1,64,1,8,128]{4,1,3,2,0:T(8,128)(2,1)S(1)} %get-tuple-element.19), channel_id=1, source_target_pairs={{0,4},{4,8},{8,12},{1,5},{5,9},{9,13},{2,6},{6,10},{10,14},{3,7},{... | collective-permute-start | bytes 393224 | tf_op jit(solution)/shard_map/ppermute | solution.py:18
  45.8 1.3 collective-permute-start.5
  47.8 3.8 collective-permute-done.5
  51.6 3.3 collective-permute-start.6
  54.9 1.9 collective-permute-start.7
  57.5 5.1 %collective-permute-start.10 = (bf16[1,128,4,1,128]{4,1,3,2,0:T(8,128)(2,1)S(1)}, bf16[1,128,4,1,128]{4,1,3,2,0:T(8,128)(2,1)S(1)}, u32[]{:S(2)}, u32[]{:S(2)}) collective-permute-start(bf16[1,128,4,1,128]{4,1,3,2,0:T(8,128)(2,1)S(1)} %get-tuple-element.11), channel_id=1, source_target_pairs={{0,1},{1,2},{2,3},{4,5},{5,6},{6,7},{8,9},{9,10},{10,11},{12,13},{... | collective-permute-start | bytes 393224 | tf_op jit(solution)/shard_map/ppermute | solution.py:18
  62.6 2.1 collective-permute-start.11
  65.8 0.9 fusion.85
  67.5 1.5 convolution_bitcast_fusion
  69.1 1.3 convolution_bitcast_fusion.7
  70.4 0.9 fusion.84
  71.4 1.0 fusion.83
  74.1 0.9 fusion.80
  75.1 0.9 fusion.79
  76.0 1.3 convolution_bitcast_fusion.1
  78.3 1.0 fusion.77
  80.1 0.9 fusion.75
  81.0 0.9 fusion.74
  82.0 0.9 fusion.73
  82.9 0.9 fusion.72
  83.8 0.9 fusion.71
  84.8 0.9 fusion.70
  86.6 0.9 fusion.68
  87.6 0.9 fusion.67
  88.5 0.9 fusion.66
  89.4 0.9 fusion.65
  91.2 0.9 fusion.63
  92.2 1.0 fusion.62
  93.1 0.9 fusion.61
  94.0 0.9 fusion.60
  94.9 0.9 fusion.59
  98.1 1.5 convolution_add_fusion.7
  99.6 1.3 convolution_bitcast_fusion.2
  100.9 1.4 convolution_bitcast_fusion.3
  102.4 1.7 fusion.5
  117.7 1.8 copy.63
  119.6 2.1 convolution_bitcast_fusion.5
  121.7 4.0 copy.91
  125.7 2.3 convolution_bitcast_fusion.6
  128.1 2.1 convolution_add_fusion.6
  130.5 2.1 convolution_bitcast_fusion.8
  132.6 2.2 convolution_bitcast_fusion.9
  134.8 1.3 convolution_add_fusion.5
  136.1 1.2 convolution_add_fusion.4
  137.3 1.1 convolution_add_fusion.3
  138.4 1.1 convolution_add_fusion.2
  139.4 1.2 convolution_add_fusion.1
  140.6 1.1 fusion.7
  141.7 41.0 %reduce-scatter.3.cloned.1.call-done = f32[27,4,32]{2,0,1:T(8,128)} async-done(((f32[27,64,32]{2,0,1:T(8,128)}), f32[27,4,32]{2,0,1:T(8,128)}) %reduce-scatter.3.cloned.1.call-update) | async-done | bytes 13840 | tf_op jit(solution)/shard_map/reduce_scatter | solution.py:83
  182.7 75.2 %reduce-scatter.5.cloned.1.call-done = f32[27,8,64]{2,0,1:T(8,128)} async-done(((f32[27,128,64]{2,0,1:T(8,128)}), f32[27,8,64]{2,0,1:T(8,128)}) %reduce-scatter.5.cloned.1.call-update) | async-done | bytes 55312 | tf_op jit(solution)/shard_map/reduce_scatter | solution.py:84
  257.9 4.5 %fusion.27 = bf16[1,128,2,8,128]{1,4,3,2,0:T(8,128)(2,1)S(1)} fusion(f32[1,128,2,8,128]{1,4,3,2,0:T(8,128)} %convolution_bitcast_fusion, f32[1,128,2,8,128]{1,4,3,2,0:T(8,128)} %convolution_bitcast_fusion.1, f32[1,128,2,8,128]{1,4,3,2,0:T(8,128)} %convolution_bitcast_fusion.2, f32[1,128,2,8,128]{1,4,3,2,0:T(8,128)} %convolution_bitcast_fusion.3, ...), kind=kOutput, calls=%fused_computation.64 | convolution fusion | flops 36700160 | bytes 12337152 | tf_op jit(solution)/shard_map/oi,bidhw->bodhw/dot_general | solution.py:43
  262.5 1.2 copy.92
  263.7 144.2 %all-reduce.6.cloned.1.call-done = (f32[27,4,32]{2,0,1:T(8,128)}, f32[27,8,64]{2,0,1:T(8,128)}) async-done(((f32[27,4,32]{2,0,1:T(8,128)}, f32[27,8,64]{2,0,1:T(8,128)}), (f32[27,4,32]{2,0,1:T(8,128)}, f32[27,8,64]{2,0,1:T(8,128)})) %all-reduce.6.cloned.1.call-update) | async-done | bytes 69136 | tf_op jit(solution)/shard_map/psum | solution.py:81
  407.9 1.6 copy.94
  409.5 1.5 copy.93
  (143 shorter events, 33.1 us)
Async XLA Ops:
  7.2 175.6 %reduce-scatter.3.cloned.1.call-start = ((), (), s32[]{:S(2)}) async-start(), calls=%async_computation.2 | async-start | bytes 1114112 | tf_op jit(solution)/shard_map/reduce_scatter | solution.py:83
  8.2 12.1 %copy-start.5 = (bf16[1,32,2,8,128]{4,3,2,1,0:T(8,128)(2,1)S(1)}, bf16[1,32,2,8,128]{4,3,2,1,0:T(8,128)(2,1)}, u32[]{:S(2)}) copy-start(bf16[1,32,2,8,128]{4,3,2,1,0:T(8,128)(2,1)} %param.4) | copy-start | bytes 393220
  8.2 12.1 %collective-permute-start = (bf16[1,32,1,8,128]{4,1,3,2,0:T(8,128)(2,1)S(1)}, bf16[1,32,1,8,128]{4,1,3,2,0:T(8,128)(2,1)S(1)}, u32[]{:S(2)}, u32[]{:S(2)}) collective-permute-start(bf16[1,32,1,8,128]{4,1,3,2,0:T(8,128)(2,1)S(1)} %get-tuple-element.24), channel_id=1, source_target_pairs={{0,4},{4,8},{8,12},{1,5},{5,9},{9,13},{2,6},{6,10},{10,14},{3,7},{... | collective-permute-start | bytes 196616 | tf_op jit(solution)/shard_map/ppermute | solution.py:18
  12.3 16.3 %copy-start.7 = (bf16[27,64,32]{1,2,0:T(8,128)(2,1)S(1)}, bf16[27,64,32]{1,2,0:T(8,128)(2,1)}, u32[]{:S(2)}) copy-start(bf16[27,64,32]{1,2,0:T(8,128)(2,1)} %param.5) | copy-start | bytes 331780
  12.3 8.1 %collective-permute-start.1 = (bf16[1,32,1,8,128]{4,1,3,2,0:T(8,128)(2,1)S(1)}, bf16[1,32,1,8,128]{4,1,3,2,0:T(8,128)(2,1)S(1)}, u32[]{:S(2)}, u32[]{:S(2)}) collective-permute-start(bf16[1,32,1,8,128]{4,1,3,2,0:T(8,128)(2,1)S(1)} %get-tuple-element.23), channel_id=1, source_target_pairs={{4,0},{8,4},{12,8},{5,1},{9,5},{13,9},{6,2},{10,6},{14,10},{7,3},{... | collective-permute-start | bytes 196616 | tf_op jit(solution)/shard_map/ppermute | solution.py:19
  14.9 42.2 %collective-permute-start.8 = (bf16[1,128,1,8,128]{4,1,3,2,0:T(8,128)(2,1)S(1)}, bf16[1,128,1,8,128]{4,1,3,2,0:T(8,128)(2,1)S(1)}, u32[]{:S(2)}, u32[]{:S(2)}) collective-permute-start(bf16[1,128,1,8,128]{4,1,3,2,0:T(8,128)(2,1)S(1)} %get-tuple-element.14), channel_id=1, source_target_pairs={{0,4},{4,8},{8,12},{1,5},{5,9},{9,13},{2,6},{6,10},{10,14},{3,7},{... | collective-permute-start | bytes 786440 | tf_op jit(solution)/shard_map/ppermute | solution.py:18
  19.0 38.4 %collective-permute-start.9 = (bf16[1,128,1,8,128]{4,1,3,2,0:T(8,128)(2,1)S(1)}, bf16[1,128,1,8,128]{4,1,3,2,0:T(8,128)(2,1)S(1)}, u32[]{:S(2)}, u32[]{:S(2)}) collective-permute-start(bf16[1,128,1,8,128]{4,1,3,2,0:T(8,128)(2,1)S(1)} %get-tuple-element.13), channel_id=1, source_target_pairs={{4,0},{8,4},{12,8},{5,1},{9,5},{13,9},{6,2},{10,6},{14,10},{7,3},{... | collective-permute-start | bytes 786440 | tf_op jit(solution)/shard_map/ppermute | solution.py:19
  20.4 8.4 %collective-permute-start.2 = (bf16[1,32,4,1,128]{4,1,3,2,0:T(8,128)(2,1)S(1)}, bf16[1,32,4,1,128]{4,1,3,2,0:T(8,128)(2,1)S(1)}, u32[]{:S(2)}, u32[]{:S(2)}) collective-permute-start(bf16[1,32,4,1,128]{4,1,3,2,0:T(8,128)(2,1)S(1)} %get-tuple-element.21), channel_id=1, source_target_pairs={{0,1},{1,2},{2,3},{4,5},{5,6},{6,7},{8,9},{9,10},{10,11},{12,13},{... | collective-permute-start | bytes 98312 | tf_op jit(solution)/shard_map/ppermute | solution.py:18
  26.6 6.7 %collective-permute-start.3 = (bf16[1,32,4,1,128]{4,1,3,2,0:T(8,128)(2,1)S(1)}, bf16[1,32,4,1,128]{4,1,3,2,0:T(8,128)(2,1)S(1)}, u32[]{:S(2)}, u32[]{:S(2)}) collective-permute-start(bf16[1,32,4,1,128]{4,1,3,2,0:T(8,128)(2,1)S(1)} %get-tuple-element.22), channel_id=1, source_target_pairs={{1,0},{2,1},{3,2},{5,4},{6,5},{7,6},{9,8},{10,9},{11,10},{13,12},{... | collective-permute-start | bytes 98312 | tf_op jit(solution)/shard_map/ppermute | solution.py:19
  40.9 6.2 %copy-start = (bf16[1,128,2,8,128]{4,3,2,1,0:T(8,128)(2,1)S(1)}, bf16[1,128,2,8,128]{4,3,2,1,0:T(8,128)(2,1)}, u32[]{:S(2)}) copy-start(bf16[1,128,2,8,128]{4,3,2,1,0:T(8,128)(2,1)} %param.7) | copy-start | bytes 1572868
  40.9 6.2 %copy-start.6 = (bf16[27,128,64]{1,2,0:T(8,128)(2,1)S(1)}, bf16[27,128,64]{1,2,0:T(8,128)(2,1)}, u32[]{:S(2)}) copy-start(bf16[27,128,64]{1,2,0:T(8,128)(2,1)} %param.6) | copy-start | bytes 1327108
  41.6 6.2 %collective-permute-start.4 = (bf16[1,64,1,8,128]{4,1,3,2,0:T(8,128)(2,1)S(1)}, bf16[1,64,1,8,128]{4,1,3,2,0:T(8,128)(2,1)S(1)}, u32[]{:S(2)}, u32[]{:S(2)}) collective-permute-start(bf16[1,64,1,8,128]{4,1,3,2,0:T(8,128)(2,1)S(1)} %get-tuple-element.19), channel_id=1, source_target_pairs={{0,4},{4,8},{8,12},{1,5},{5,9},{9,13},{2,6},{6,10},{10,14},{3,7},{... | collective-permute-start | bytes 393224 | tf_op jit(solution)/shard_map/ppermute | solution.py:18
  45.8 5.7 %collective-permute-start.5 = (bf16[1,64,1,8,128]{4,1,3,2,0:T(8,128)(2,1)S(1)}, bf16[1,64,1,8,128]{4,1,3,2,0:T(8,128)(2,1)S(1)}, u32[]{:S(2)}, u32[]{:S(2)}) collective-permute-start(bf16[1,64,1,8,128]{4,1,3,2,0:T(8,128)(2,1)S(1)} %get-tuple-element.20), channel_id=1, source_target_pairs={{4,0},{8,4},{12,8},{5,1},{9,5},{13,9},{6,2},{10,6},{14,10},{7,3},{... | collective-permute-start | bytes 393224 | tf_op jit(solution)/shard_map/ppermute | solution.py:19
  51.6 13.4 %collective-permute-start.6 = (bf16[1,64,4,1,128]{4,1,3,2,0:T(8,128)(2,1)S(1)}, bf16[1,64,4,1,128]{4,1,3,2,0:T(8,128)(2,1)S(1)}, u32[]{:S(2)}, u32[]{:S(2)}) collective-permute-start(bf16[1,64,4,1,128]{4,1,3,2,0:T(8,128)(2,1)S(1)} %get-tuple-element.17), channel_id=1, source_target_pairs={{0,1},{1,2},{2,3},{4,5},{5,6},{6,7},{8,9},{9,10},{10,11},{12,13},{... | collective-permute-start | bytes 196616 | tf_op jit(solution)/shard_map/ppermute | solution.py:18
  54.9 10.1 %collective-permute-start.7 = (bf16[1,64,4,1,128]{4,1,3,2,0:T(8,128)(2,1)S(1)}, bf16[1,64,4,1,128]{4,1,3,2,0:T(8,128)(2,1)S(1)}, u32[]{:S(2)}, u32[]{:S(2)}) collective-permute-start(bf16[1,64,4,1,128]{4,1,3,2,0:T(8,128)(2,1)S(1)} %get-tuple-element.18), channel_id=1, source_target_pairs={{1,0},{2,1},{3,2},{5,4},{6,5},{7,6},{9,8},{10,9},{11,10},{13,12},{... | collective-permute-start | bytes 196616 | tf_op jit(solution)/shard_map/ppermute | solution.py:19
  57.5 44.9 %collective-permute-start.10 = (bf16[1,128,4,1,128]{4,1,3,2,0:T(8,128)(2,1)S(1)}, bf16[1,128,4,1,128]{4,1,3,2,0:T(8,128)(2,1)S(1)}, u32[]{:S(2)}, u32[]{:S(2)}) collective-permute-start(bf16[1,128,4,1,128]{4,1,3,2,0:T(8,128)(2,1)S(1)} %get-tuple-element.11), channel_id=1, source_target_pairs={{0,1},{1,2},{2,3},{4,5},{5,6},{6,7},{8,9},{9,10},{10,11},{12,13},{... | collective-permute-start | bytes 393224 | tf_op jit(solution)/shard_map/ppermute | solution.py:18
  62.6 39.7 %collective-permute-start.11 = (bf16[1,128,4,1,128]{4,1,3,2,0:T(8,128)(2,1)S(1)}, bf16[1,128,4,1,128]{4,1,3,2,0:T(8,128)(2,1)S(1)}, u32[]{:S(2)}, u32[]{:S(2)}) collective-permute-start(bf16[1,128,4,1,128]{4,1,3,2,0:T(8,128)(2,1)S(1)} %get-tuple-element.12), channel_id=1, source_target_pairs={{1,0},{2,1},{3,2},{5,4},{6,5},{7,6},{9,8},{10,9},{11,10},{13,12},{... | collective-permute-start | bytes 393224 | tf_op jit(solution)/shard_map/ppermute | solution.py:19
  69.1 26.8 %copy-start.4 = (bf16[1,64,4,9,128]{4,1,3,2,0:T(8,128)(2,1)}, bf16[1,64,4,9,128]{4,1,3,2,0:T(8,128)(2,1)S(1)}, u32[]{:S(2)}) copy-start(bf16[1,64,4,9,128]{4,1,3,2,0:T(8,128)(2,1)S(1)} %get-tuple-element.15) | copy-start | bytes 1769476
  69.1 28.7 %copy-start.3 = (bf16[1,64,4,9,128]{4,1,3,2,0:T(8,128)(2,1)}, bf16[1,64,4,9,128]{4,1,3,2,0:T(8,128)(2,1)S(1)}, u32[]{:S(2)}) copy-start(bf16[1,64,4,9,128]{4,1,3,2,0:T(8,128)(2,1)S(1)} %get-tuple-element.16) | copy-start | bytes 1769476
  119.5 138.4 %reduce-scatter.5.cloned.1.call-start = ((), (), s32[]{:S(2)}) async-start(), calls=%async_computation.3 | async-start | bytes 2228224 | tf_op jit(solution)/shard_map/reduce_scatter | solution.py:84
  125.7 2.3 copy-start.1
  130.1 277.7 %all-reduce.6.cloned.1.call-start = ((), (), s32[]{:S(2)}) async-start(), calls=%async_computation.4 | async-start | bytes 393216 | tf_op jit(solution)/shard_map/psum | solution.py:81
  130.5 4.3 %copy-start.2 = (f32[2,8,128,128]{3,2,1,0:T(8,128)S(1)}, f32[2,8,128,128]{3,2,1,0:T(8,128)}, u32[]{:S(2)}) copy-start(f32[2,8,128,128]{3,2,1,0:T(8,128)} %convolution_add_fusion.6) | copy-start | bytes 3145732
Sparse Core Ops, SparseCore 0:
  119.6 63.0 reduce-scatter.2
  185.4 72.4 reduce-scatter.4
  260.8 147.0 all-reduce.5
where the time goes:
time: 419 us; the launch traced here: 418 us
  waiting for transfers between devices  269 us (64%)
  matrix products  80.8 us (19%)
  starting transfers between devices  37.4 us (9%)
  between operations  14.5 us (3%)
  local copies, waits for them, and re-layouts  12.7 us (3%)
    psum x1, waiting for transfers between devices, per_device(): summed = lax.psum((grad_first, grad_second), ('dep', 'hgt'))  144 us
    reduce_scatter x1, waiting for transfers between devices, per_device(): lax.psum_scatter(summed[1], 'dp', scatter_dimension=1, tiled=True)  75.2 us
    dot_general x54, matrix products, convolve(): jnp.einsum('oi,bidhw->bodhw', kernel[number], piece, preferred_element_ty...  41.9 us
    reduce_scatter x1, waiting for transfers between devices, per_device(): lax.psum_scatter(summed[0], 'dp', scatter_dimension=1, tiled=True)  41 us
    dot_general x54, matrix products, kernel_grad(): jnp.einsum('bodhw,bidhw->oi', upstream, piece, preferred_element_type=jnp...  31.1 us
    ppermute x6, starting transfers between devices, extended_2(): before = lax.ppermute(last, axis, up)  27.1 us
    ppermute x6, starting transfers between devices, extended_2(): after = lax.ppermute(leading, axis, down)  9.95 us
  transfers between devices with their start and end apart: 15, of which 6 were waited for; matrix products, arithmetic and copies ran while one was open for 18% of the time, Pallas kernels for 0%

commit v1 on v0

v1 whole, which is shorter than its diff:
```python
import functools

import jax
import jax.numpy as jnp
from jax import lax
from jax.experimental import pallas as pl
from jax.experimental.pallas import tpu as pltpu
from jax.sharding import PartitionSpec as P

MESH = pl.DeviceIdType.MESH
BF = jnp.bfloat16
F32 = jnp.float32
W = 128
DIRS = [(a, b) for a in (-1, 0, 1) for b in (-1, 0, 1) if (a, b) != (0, 0)]
NT = (((1,), (1,)), ((), ()))


def dot(a, b):
    return jnp.dot(a, b, preferred_element_type=F32)


def shifted(x, by):
    if by == 0:
        return x
    lane = lax.broadcasted_iota(jnp.int32, x.shape, 1)
    keep = lane >= by if by > 0 else lane < W + by
    return jnp.where(keep, pltpu.roll(x, by % W, 1), 0.0)


def pair(ref, d, h, rows):
    halves = [ref[d + e, pl.ds(h, 3)].reshape(rows, W) for e in (0, 1)]
    return jnp.concatenate(halves, axis=1)


def kernel(
    sizes,
    vol,
    k1t,
    k2t,
    cot,
    feat,
    g1_out,
    g2_out,
    V,
    C,
    tmp,
    W1,
    W2,
    WB,
    BS,
    BO,
    RBX,
    RBH,
    RBD,
    H,
    H3,
    DS,
    D3,
    G,
    GB,
    RC,
    ZS,
    RZ,
    RY,
    RX,
    FS,
    FO,
    v_send,
    v_recv,
    b_send,
    b_recv,
    c_send,
    c_recv,
    z_send,
    z_recv,
    y_send,
    y_recv,
    x_send,
    x_recv,
    f_send,
    f_recv,
):
    n_z, n_y, n_dep, n_hgt = sizes
    rows = 128 // n_z
    dp, dep, hgt = (lax.axis_index(name) for name in ("dp", "dep", "hgt"))
    z, yl = dp // 2, dp % 2
    yh, core = hgt // 2, hgt % 2
    y = yh * 2 + yl

    def there(direction, sign):
        d, h = dep + sign * direction[0], hgt + sign * direction[1]
        return (d >= 0) & (d < n_dep) & (h >= 0) & (h < n_hgt)

    def z_peer(m):
        return (((z + m) % n_z) * 2 + yl, dep, hgt)

    def y_peer(m):
        other = (y + m) % n_y
        return (z * 2 + other % 2, dep, (other // 2) * 2 + core)

    def x_peer(m):
        return (dp, (dep + m) % n_dep, hgt)

    partner = (dp, dep, hgt + 1 - 2 * core)

    V[...] = jnp.zeros_like(V)
    RBX[...] = jnp.zeros_like(RBX)
    RBH[...] = jnp.zeros_like(RBH)
    RBD[...] = jnp.zeros_like(RBD)

    barrier = pltpu.get_barrier_semaphore()
    for direction in DIRS:

        @pl.when(there(direction, 1))
        def _():
            pl.semaphore_signal(
                barrier,
                inc=1,
                device_id=(dp, dep + direction[0], hgt + direction[1]),
                device_id_type=MESH,
            )

    peers = [partner]
    peers += [z_peer(m) for m in range(1, n_z)]
    peers += [y_peer(m) for m in range(1, n_y)]
    peers += [x_peer(m) for m in range(1, n_dep)]
    for peer in peers:
        pl.semaphore_signal(barrier, inc=1, device_id=peer, device_id_type=MESH)

    for d in (0, 1):
        tmp[0:256, :] = vol[:, d].astype(F32).reshape(256, W)
        for h in range(8):
            V[2 + d, 2 + h] = tmp[pl.ds(h, 32, stride=8), :].astype(BF)

    span_d = 1 + (dep > 0).astype(jnp.int32) + (dep < n_dep - 1).astype(jnp.int32)
    span_h = 1 + (hgt > 0).astype(jnp.int32) + (hgt < n_hgt - 1).astype(jnp.int32)
    pl.semaphore_wait(barrier, span_d * span_h - 1 + len(peers))

    def v_copy(k):
        a, b = DIRS[k]
        to_d = {0: (2, 4), 1: (0, 2), -1: (4, 6)}[a]
        from_h, to_h = {0: ((2, 10), (2, 10)), 1: ((8, 10), (0, 2)), -1: ((2, 4), (10, 12))}[b]
        return pltpu.make_async_remote_copy(
            src_ref=V.at[2:4, from_h[0] : from_h[1]],
            dst_ref=V.at[to_d[0] : to_d[1], to_h[0] : to_h[1]],
            send_sem=v_send.at[k],
            recv_sem=v_recv.at[k],
            device_id=(dp, dep + a, hgt + b),
            device_id_type=MESH,
        )

    def b_copy(k):
        a, b = DIRS[k]
        d = {-1: 0, 1: 3}.get(a)
        h = {-1: 0, 1: 9}.get(b)
        if a == 0:
            src, dst = BS.at[1:3, h], RBH.at[(b + 1) // 2]
        elif b == 0:
            src, dst = BS.at[d, 1:9], RBX.at[(a + 1) // 2]
        else:
            src, dst = BS.at[d, h], RBD.at[(a + 1) + (b + 1) // 2]
        return pltpu.make_async_remote_copy(
            src_ref=src,
            dst_ref=dst,
            send_sem=b_send.at[k],
            recv_sem=b_recv.at[k],
            device_id=(dp, dep + a, hgt + b),
            device_id_type=MESH,
        )

    def halo(copy, sign, what):
        for k, direction in enumerate(DIRS):

            @pl.when(there(direction, sign))
            def _():
                getattr(copy(k), what)()

    halo(v_copy, 1, "start")

    for d in (0, 1):
        for h in (0, 1, 10, 11):
            C[d, h] = jnp.zeros((128, W), BF)
        tmp[...] = cot[:, d].astype(F32).reshape(1024, W)

        @pl.loop(0, 8)
        def _(h):
            C[d, 2 + h] = tmp[pl.ds(h, 128, stride=8), :].astype(BF)

    for a in range(3):
        for b in range(3):
            for c in range(3):
                WB[a * 192 + c * 64 : a * 192 + c * 64 + 64, (2 - b) * 128 : (3 - b) * 128] = k2t[
                    9 * a + 3 * b + c
                ]

    @pl.loop(0, 10)
    def _(h):
        t = dot(WB[...], pair(C, 0, h, 384))
        sums = []
        for a in range(3):
            halves = []
            for e in (0, 1):
                parts = [
                    shifted(t[a * 192 + c * 64 : a * 192 + c * 64 + 64, e * W : e * W + W], c - 1)
                    for c in range(3)
                ]
                halves.append(parts[0] + parts[1] + parts[2])
            sums.append(halves)
        inner = [sums[0][1] + sums[1][0], sums[1][1] + sums[2][0]]
        BS[0, h] = sums[0][0].astype(BF)
        BS[3, h] = sums[2][1].astype(BF)
        for d in (0, 1):
            BS[1 + d, h] = inner[d].astype(BF)
            BO[d, h] = inner[d]

    halo(b_copy, 1, "start")

    for c in range(3):
        stack = [k1t[3 * t + c].astype(F32) for t in range(9)]
        W1[c * 64 : c * 64 + 64, :] = jnp.concatenate(stack, axis=0).T.astype(BF)

    halo(v_copy, -1, "wait_recv")

    @pl.loop(0, 10)
    def _(h):
        ok_h = ((h > 0) | (hgt > 0)) & ((h < 9) | (hgt < n_hgt - 1))
        for d in (0, 2):
            x = jnp.concatenate([pair(V, d + a, h, 96) for a in range(3)], axis=0)
            t = dot(W1[...], x)
            for e in (0, 1):
                part = [t[c * 64 : c * 64 + 64, e * W : e * W + W] for c in range(3)]
                pre = shifted(part[0], 1) + part[1] + shifted(part[2], -1)
                sigma = 1.0 / (1.0 + jnp.exp(-pre))
                ok = ok_h
                if d + e == 0:
                    ok = ok & (dep > 0)
                elif d + e == 3:
                    ok = ok & (dep < n_dep - 1)
                hid = pre * sigma * ok.astype(F32)
                H[d + e, h] = hid.astype(BF)
                for c in range(3):
                    H3[d + e, h, c * 64 : c * 64 + 64] = shifted(hid, 1 - c).astype(BF)
                if d + e in (1, 2):
                    DS[d + e - 1, h] = sigma * (1.0 + pre * (1.0 - sigma))

    def keep(owner, unit, value):
        value = value.reshape(n_z, rows, W)
        G[owner, :, unit] = value
        GB[owner, :, unit] = value.astype(BF)

    upstream = [C[d, 2 + h] for h in range(8) for d in (0, 1)]
    upstream = jnp.concatenate(upstream, axis=1)
    lasts = {}
    for a in range(3):
        for b in range(3):
            field = [H3[d + a, h + b] for h in range(8) for d in (0, 1)]
            part = lax.dot_general(
                upstream, jnp.concatenate(field, axis=1), NT, preferred_element_type=F32
            )
            keep(0, 3 * a + b, part[:, :128])
            lasts[a, b] = part[:, 128:192]
        keep(1, a, jnp.concatenate([lasts[a, 0], lasts[a, 1]], axis=1))
    keep(1, 3, jnp.concatenate([lasts[0, 2], lasts[1, 2]], axis=1))
    keep(1, 4, jnp.concatenate([lasts[2, 2], jnp.zeros((128, 64), F32)], axis=1))

    halo(b_copy, -1, "wait_recv")

    for d, a in ((0, 1), (1, -1)):
        for h, b in ((0, 1), (7, -1)):
            BO[d, 1 + h] += RBH[(b + 1) // 2, d].astype(F32) + RBD[(a + 1) + (b + 1) // 2].astype(F32)

    @pl.loop(0, 8)
    def _(h):
        for d, a in ((0, 1), (1, -1)):
            back = BO[d, 1 + h] + RBX[(a + 1) // 2, h].astype(F32)
            delta = back * DS[d, 1 + h]
            for c in range(3):
                D3[2 * h + d, c * 64 : c * 64 + 64] = shifted(delta, c - 1).astype(BF)

    upstream = jnp.concatenate([D3[r] for r in range(16)], axis=1)
    field = [
        jnp.concatenate(
            [V[2 + d + a - 1, 2 + h - 1 : 2 + h + 2].reshape(96, W) for a in range(3)], axis=0
        )
        for h in range(8)
        for d in (0, 1)
    ]
    part = lax.dot_general(
        upstream, jnp.concatenate(field, axis=1), NT, preferred_element_type=F32
    )
    blocks = [part[c * 64 : c * 64 + 64, j * W : j * W + W] for c in range(3) for j in (0, 1)]
    ends = [part[c * 64 : c * 64 + 64, 256:288] for c in range(3)]
    blocks.append(jnp.concatenate(ends + [jnp.zeros((64, 32), F32)], axis=1))
    blocks.append(jnp.zeros((64, W), F32))
    for m in range(4):
        two = [blocks[2 * m + e].reshape(n_z, rows // 2, W) for e in (0, 1)]
        value = jnp.concatenate(two, axis=1)
        G[1, :, 5 + m] = value
        GB[1, :, 5 + m] = value.astype(BF)

    c_copy = pltpu.make_async_remote_copy(
        src_ref=GB.at[1 - core],
        dst_ref=RC,
        send_sem=c_send,
        recv_sem=c_recv,
        device_id=partner,
        device_id_type=MESH,
    )
    c_copy.start()
    for c in range(3):
        stack = [k2t[3 * t + c].astype(F32) for t in range(9)]
        W2[c * 128 : c * 128 + 128, :] = jnp.concatenate(stack, axis=0).T.astype(BF)
    c_copy.wait()

    @pl.loop(0, n_z)
    def _(j):
        ZS[j] = (G[core, j] + RC[j].astype(F32)).astype(BF)

    def z_copy(m):
        return pltpu.make_async_remote_copy(
            src_ref=ZS.at[(z + m) % n_z],
            dst_ref=RZ.at[m],
            send_sem=z_send.at[m],
            recv_sem=z_recv.at[m],
            device_id=z_peer(m),
            device_id_type=MESH,
        )

    for m in range(1, n_z):
        z_copy(m).start()

    @pl.loop(0, 8)
    def _(h):
        x = jnp.concatenate([pair(H, a, h, 192) for a in range(3)], axis=0)
        t = dot(W2[...], x)
        for d in (0, 1):
            part = [t[c * 128 : c * 128 + 128, d * W : d * W + W] for c in range(3)]
            total = shifted(part[0], 1) + part[1] + shifted(part[2], -1)
            FO[d, pl.ds(h, 128, stride=8), :] = total

    for d in (0, 1):
        feat[:, d] = FO[d].reshape(128, 8, W).astype(BF)

    for m in range(1, n_z):
        z_copy(m).wait()
    total = G[core, z] + RC[z].astype(F32)
    for m in range(1, n_z):
        total = total + RZ[m].astype(F32)
    RY[y] = total.astype(BF)

    def y_copy(m):
        return pltpu.make_async_remote_copy(
            src_ref=RY.at[y],
            dst_ref=RY.at[y],
            send_sem=y_send.at[m],
            recv_sem=y_recv.at[m],
            device_id=y_peer(m),
            device_id_type=MESH,
        )

    def y_wait(m):
        other = (y + n_y - m) % n_y
        return pltpu.make_async_remote_copy(
            src_ref=RY.at[y],
            dst_ref=RY.at[other],
            send_sem=y_send.at[m],
            recv_sem=y_recv.at[m],
            device_id=y_peer(m),
            device_id_type=MESH,
        )

    for m in range(1, n_y):
        y_copy(m).start()
    for m in range(1, n_y):
        y_wait(m).wait()
    total = RY[0].astype(F32)
    for m in range(1, n_y):
        total = total + RY[m].astype(F32)
    RX[dep] = total.astype(BF)

    def x_copy(m):
        return pltpu.make_async_remote_copy(
            src_ref=RX.at[dep],
            dst_ref=RX.at[dep],
            send_sem=x_send.at[m],
            recv_sem=x_recv.at[m],
            device_id=x_peer(m),
            device_id_type=MESH,
        )

    def x_wait(m):
        other = (dep + n_dep - m) % n_dep
        return pltpu.make_async_remote_copy(
            src_ref=RX.at[dep],
            dst_ref=RX.at[other],
            send_sem=x_send.at[m],
            recv_sem=x_recv.at[m],
            device_id=x_peer(m),
            device_id_type=MESH,
        )

    for m in range(1, n_dep):
        x_copy(m).start()
    for m in range(1, n_dep):
        x_wait(m).wait()
    total = RX[0].astype(F32)
    for m in range(1, n_dep):
        total = total + RX[m].astype(F32)
    FS[core] = total

    def f_copy(slot):
        return pltpu.make_async_remote_copy(
            src_ref=FS.at[core],
            dst_ref=FS.at[slot],
            send_sem=f_send,
            recv_sem=f_recv,
            device_id=partner,
            device_id_type=MESH,
        )

    f_copy(core).start()
    f_copy(1 - core).wait()

    half = rows // 2
    for t in range(9):
        got = FS[0, t, pl.ds(pl.multiple_of(yl * half, half), half), :]
        g2_out[3 * t] = got[:, :64]
        g2_out[3 * t + 1] = got[:, 64:]
    taps = [(a, b) for a in range(3) for b in (0, 1)] + [(0, 2), (1, 2), (2, 2)]
    for n, (a, b) in enumerate(taps):
        got = FS[1, n // 2, pl.ds(pl.multiple_of(yl * half, half), half), :]
        g2_out[9 * a + 3 * b + 2] = got[:, (n % 2) * 64 : (n % 2) * 64 + 64]
    own = half // 2
    for block in range(7):
        both = FS[1, 5 + block // 2, (block % 2) * half : (block % 2) * half + half, :]
        got = jnp.where(yl == 0, both[:own], both[own:])
        for n in range(4 if block < 6 else 3):
            lanes = got[:, n * 32 : n * 32 + 32]
            if block < 6:
                g1_out[3 * (4 * (block % 2) + n) + block // 2] = lanes
            else:
                g1_out[24 + n] = lanes

    halo(v_copy, 1, "wait_send")
    halo(b_copy, 1, "wait_send")


def per_device(sizes, volume, kernel_first, kernel_second, cotangent):
    n_z, n_y, n_dep, n_hgt = sizes
    rows = 128 // n_z
    vmem = pl.BlockSpec(memory_space=pltpu.VMEM)
    dma = pltpu.SemaphoreType.DMA
    features, grad_first, grad_second = pl.pallas_call(
        functools.partial(kernel, sizes),
        out_shape=(
            jax.ShapeDtypeStruct((128, 2, 8, W), BF),
            jax.ShapeDtypeStruct((27, rows // 4, 32), F32),
            jax.ShapeDtypeStruct((27, rows // 2, 64), F32),
        ),
        in_specs=[vmem] * 4,
        out_specs=(vmem, vmem, vmem),
        scratch_shapes=[
            pltpu.VMEM((6, 12, 32, W), BF),
            pltpu.VMEM((2, 12, 128, W), BF),
            pltpu.VMEM((1024, W), F32),
            pltpu.VMEM((192, 288), BF),
            pltpu.VMEM((384, 576), BF),
            pltpu.VMEM((576, 384), BF),
            pltpu.VMEM((4, 10, 64, W), BF),
            pltpu.VMEM((2, 10, 64, W), F32),
            pltpu.VMEM((2, 8, 64, W), BF),
            pltpu.VMEM((2, 2, 64, W), BF),
            pltpu.VMEM((4, 64, W), BF),
            pltpu.VMEM((4, 10, 64, W), BF),
            pltpu.VMEM((4, 10, 192, W), BF),
            pltpu.VMEM((2, 10, 64, W), F32),
            pltpu.VMEM((16, 192, W), BF),
            pltpu.VMEM((2, n_z, 9, rows, W), F32),
            pltpu.VMEM((2, n_z, 9, rows, W), BF),
            pltpu.VMEM((n_z, 9, rows, W), BF),
            pltpu.VMEM((n_z, 9, rows, W), BF),
            pltpu.VMEM((n_z, 9, rows, W), BF),
            pltpu.VMEM((n_y, 9, rows, W), BF),
            pltpu.VMEM((n_dep, 9, rows, W), BF),
            pltpu.VMEM((2, 9, rows, W), F32),
            pltpu.VMEM((2, 1024, W), F32),
            dma((8,)),
            dma((8,)),
            dma((8,)),
            dma((8,)),
            dma,
            dma,
            dma((n_z,)),
            dma((n_z,)),
            dma((n_y,)),
            dma((n_y,)),
            dma((n_dep,)),
            dma((n_dep,)),
            dma,
            dma,
        ],
        compiler_params=pltpu.CompilerParams(
            collective_id=0, has_side_effects=True, vmem_limit_bytes=50 * 1024 * 1024
        ),
    )(
        volume[0],
        kernel_first.swapaxes(1, 2),
        kernel_second.swapaxes(1, 2),
        cotangent[0],
    )
    return features[None], grad_first, grad_second


def solution(mesh):
    placed = (P("dp", None, "dep", "hgt", None), P(), P(), P("dp", None, "dep", "hgt", None))
    shape = mesh.shape
    sizes = (shape["dp"] // 2, shape["hgt"] // 2 * 2, shape["dep"], shape["hgt"])
    return jax.shard_map(
        functools.partial(per_device, sizes),
        mesh=mesh,
        in_specs=placed,
        out_specs=(P("dp", None, "dep", "hgt", None), P(None, "dp", None), P(None, "dp", None)),
        check_vma=False,
    )
```

time: 419 us -> 53.9 us (0.13)
  waiting for transfers between devices: 269 us -> 0 us
  matrix products: 80.8 us -> 0 us
  Pallas kernels: 0 us -> 47.1 us
  starting transfers between devices: 37.4 us -> 0 us
  between operations: 14.5 us -> 0.65 us
  local copies, waits for them, and re-layouts: 12.7 us -> 5.95 us
    psum x1 -> x0, waiting for transfers between devices: 144 us -> none  [per_device(): summed = lax.psum((grad_first, grad_second), ('dep', 'hgt'))]
    reduce_scatter x2 -> x0, waiting for transfers between devices: 116 us -> none  [the longest x1 75.2 us: per_device(): lax.psum_scatter(summed[1], 'dp', scatter_dimension=1, tiled=True)]
    dot_general x135 -> x0, matrix products: 80.8 us -> none  [the longest x54 41.9 us: convolve(): jnp.einsum('oi,bidhw->bodhw', kernel[number], piece, preferred_element_ty...]
    pallas_call x0 -> x1, Pallas kernels: none -> 47.1 us  [per_device(): pl.pallas_call(functools.partial(kernel, sizes), out_shape=(jax.ShapeDtyp...]
    ppermute x12 -> x0, starting transfers between devices: 37 us -> none  [the longest x6 27.1 us: extended_2(): before = lax.ppermute(last, axis, up)]
    ppermute x12 -> x0, waiting for transfers between devices: 8.71 us -> none  [the longest x6 8.32 us: extended_2(): after = lax.ppermute(leading, axis, down)]
    another operation x2 -> x0, local copies, waits for them, and re-layouts: 5.83 us -> none  [kernel_grad(): return jnp.stack(parts)]
  transfers between devices with their start and end apart: 15 -> 0, of which waited for: 6 -> 0; matrix products, arithmetic and copies ran while one was open for 18% -> 0% of each run, Pallas kernels for 0% -> 0%
where the time goes in v1:
time: 53.9 us; the launch traced here: 53.7 us
  Pallas kernels  47.1 us (87%)
  local copies, waits for them, and re-layouts  5.95 us (11%)
  between operations  0.65 us (1%)
    pallas_call x1, Pallas kernels, per_device(): pl.pallas_call(functools.partial(kernel, sizes), out_shape=(jax.ShapeDtyp...  47.1 us
    unnamed x11, local copies, waits for them, and re-layouts  5.95 us

profile of v1, /device:TPU:1, one launch (start us, length us, event | category | flops | bytes accessed | tf_op | source)
XLA Modules:
  0.0 53.7 jit_solution(1449116523250419294)
XLA Ops:
  0.6 0.0 copy-start
  0.6 1.0 %copy-done = bf16[1,128,2,8,128]{4,3,2,1,0:T(8,128)(2,1)S(1)} copy-done((bf16[1,128,2,8,128]{4,3,2,1,0:T(8,128)(2,1)S(1)}, bf16[1,128,2,8,128]{4,3,2,1,0:T(8,128)(2,1)}, u32[]{:S(2)}) %copy-start) | copy-done | bytes 524312
  1.7 0.0 copy-start.1
  1.7 1.0 %copy-done.1 = bf16[27,128,64]{1,2,0:T(8,128)(2,1)S(1)} copy-done((bf16[27,128,64]{1,2,0:T(8,128)(2,1)S(1)}, bf16[27,128,64]{1,2,0:T(8,128)(2,1)}, u32[]{:S(2)}) %copy-start.1) | copy-done | bytes 442392
  2.7 0.0 copy-start.2
  2.7 0.9 %copy-done.2 = bf16[27,64,32]{1,2,0:T(8,128)(2,1)S(1)} copy-done((bf16[27,64,32]{1,2,0:T(8,128)(2,1)S(1)}, bf16[27,64,32]{1,2,0:T(8,128)(2,1)}, u32[]{:S(2)}) %copy-start.2) | copy-done | bytes 110616
  3.6 0.0 copy-start.3
  3.6 0.9 %copy-done.3 = bf16[1,32,2,8,128]{4,3,2,1,0:T(8,128)(2,1)S(1)} copy-done((bf16[1,32,2,8,128]{4,3,2,1,0:T(8,128)(2,1)S(1)}, bf16[1,32,2,8,128]{4,3,2,1,0:T(8,128)(2,1)}, u32[]{:S(2)}) %copy-start.3) | copy-done | bytes 131096
  4.5 47.1 %shard_map.67 = (bf16[128,2,8,128]{3,2,1,0:T(8,128)(2,1)S(1)}, f32[27,4,32]{2,1,0:T(4,128)S(1)}, f32[27,8,64]{2,1,0:T(8,128)S(1)}) custom-call(bf16[32,2,8,128]{3,2,1,0:T(8,128)(2,1)S(1)} %bitcast.9, bf16[27,32,64]{2,1,0:T(8,128)(2,1)S(1)} %bitcast.8, bf16[27,64,128]{2,1,0:T(8,128)(2,1)S(1)} %bitcast.7, bf16[128,2,8,128]{3,2,1,0:T(8,128)(2,1)S(1)} %bitcast.5), custom_call_target="tpu_custom_call" | custom-call | tf_op jit(solution)/shard_map/pallas_call | solution.py:453
  51.6 0.8 %copy.10 = bf16[1,128,2,8,128]{4,3,2,1,0:T(8,128)(2,1)} copy(bf16[1,128,2,8,128]{4,3,2,1,0:T(8,128)(2,1)S(1)} %bitcast.6) | data formatting | bytes 1048576
  52.4 0.6 %copy.11 = f32[27,4,32]{2,1,0:T(4,128)} copy(f32[27,4,32]{2,1,0:T(4,128)S(1)} %get-tuple-element.13) | data formatting | bytes 27648
  53.0 0.6 %copy.12 = f32[27,8,64]{2,1,0:T(8,128)} copy(f32[27,8,64]{2,1,0:T(8,128)S(1)} %get-tuple-element.14) | data formatting | bytes 110592
Async XLA Ops:
  0.6 1.0 %copy-start = (bf16[1,128,2,8,128]{4,3,2,1,0:T(8,128)(2,1)S(1)}, bf16[1,128,2,8,128]{4,3,2,1,0:T(8,128)(2,1)}, u32[]{:S(2)}) copy-start(bf16[1,128,2,8,128]{4,3,2,1,0:T(8,128)(2,1)} %param.7) | copy-start | bytes 1572868
  1.7 1.0 %copy-start.1 = (bf16[27,128,64]{1,2,0:T(8,128)(2,1)S(1)}, bf16[27,128,64]{1,2,0:T(8,128)(2,1)}, u32[]{:S(2)}) copy-start(bf16[27,128,64]{1,2,0:T(8,128)(2,1)} %param.6) | copy-start | bytes 1327108
  2.7 0.9 %copy-start.2 = (bf16[27,64,32]{1,2,0:T(8,128)(2,1)S(1)}, bf16[27,64,32]{1,2,0:T(8,128)(2,1)}, u32[]{:S(2)}) copy-start(bf16[27,64,32]{1,2,0:T(8,128)(2,1)} %param.5) | copy-start | bytes 331780
  3.6 0.9 %copy-start.3 = (bf16[1,32,2,8,128]{4,3,2,1,0:T(8,128)(2,1)S(1)}, bf16[1,32,2,8,128]{4,3,2,1,0:T(8,128)(2,1)}, u32[]{:S(2)}) copy-start(bf16[1,32,2,8,128]{4,3,2,1,0:T(8,128)(2,1)} %param.4) | copy-start | bytes 393220

commit v2 on v1

--- a/solution.py
+++ b/solution.py
@@ -34,13 +34,17 @@
 
 def kernel(
     sizes,
+    vol_hbm,
+    k1t_hbm,
+    k2t_hbm,
+    cot_hbm,
+    feat,
+    g1_out,
+    g2_out,
     vol,
     k1t,
     k2t,
     cot,
-    feat,
-    g1_out,
-    g2_out,
     V,
     C,
     tmp,
@@ -56,29 +60,51 @@
     H3,
     DS,
     D3,
-    G,
+    GA,
+    GA16,
+    RCA,
+    YSA,
+    RYA,
+    TA,
+    ZSA,
+    RZA,
+    RXA,
+    FA,
     GB,
-    RC,
-    ZS,
-    RZ,
-    RY,
-    RX,
-    FS,
+    GB16,
+    RCB,
+    ZSB,
+    RZB,
+    YSB,
+    RYB,
+    RXB,
+    FB,
     FO,
+    in_sem,
     v_send,
     v_recv,
     b_send,
     b_recv,
-    c_send,
-    c_recv,
-    z_send,
-    z_recv,
-    y_send,
-    y_recv,
-    x_send,
-    x_recv,
-    f_send,
-    f_recv,
+    ca_send,
+    ca_recv,
+    ya_send,
+    ya_recv,
+    za_send,
+    za_recv,
+    xa_send,
+    xa_recv,
+    fa_send,
+    fa_recv,
+    cb_send,
+    cb_recv,
+    zb_send,
+    zb_recv,
+    yb_send,
+    yb_recv,
+    xb_send,
+    xb_recv,
+    fb_send,
+    fb_recv,
 ):
     n_z, n_y, n_dep, n_hgt = sizes
     rows = 128 // n_z
@@ -101,7 +127,20 @@
     def x_peer(m):
         return (dp, (dep + m) % n_dep, hgt)
 
+    def y_far(m):
+        other = (y + m) % n_y
+        return (z * 2 + other % 2, dep, (other // 2) * 2 + 1 - core)
+
     partner = (dp, dep, hgt + 1 - 2 * core)
+
+    loads = [
+        pltpu.make_async_copy(src, dst, in_sem.at[n])
+        for n, (src, dst) in enumerate(
+            ((vol_hbm, vol), (cot_hbm, cot), (k2t_hbm, k2t), (k1t_hbm, k1t))
+        )
+    ]
+    for load in loads:
+        load.start()
 
     V[...] = jnp.zeros_like(V)
     RBX[...] = jnp.zeros_like(RBX)
@@ -123,14 +162,34 @@
     peers = [partner]
     peers += [z_peer(m) for m in range(1, n_z)]
     peers += [y_peer(m) for m in range(1, n_y)]
+    peers += [y_far(m) for m in range(1, n_y)]
     peers += [x_peer(m) for m in range(1, n_dep)]
     for peer in peers:
         pl.semaphore_signal(barrier, inc=1, device_id=peer, device_id_type=MESH)
 
+    loads[0].wait()
     for d in (0, 1):
         tmp[0:256, :] = vol[:, d].astype(F32).reshape(256, W)
         for h in range(8):
             V[2 + d, 2 + h] = tmp[pl.ds(h, 32, stride=8), :].astype(BF)
+
+    loads[1].wait()
+    for d in (0, 1):
+        for h in (0, 1, 10, 11):
+            C[d, h] = jnp.zeros((128, W), BF)
+        tmp[...] = cot[:, d].astype(F32).reshape(1024, W)
+
+        @pl.loop(0, 8, unroll=4)
+        def _(h):
+            C[d, 2 + h] = tmp[pl.ds(h, 128, stride=8), :].astype(BF)
+
+    loads[2].wait()
+    for a in range(3):
+        for b in range(3):
+            for c in range(3):
+                WB[a * 192 + c * 64 : a * 192 + c * 64 + 64, (2 - b) * 128 : (3 - b) * 128] = k2t[
+                    9 * a + 3 * b + c
+                ]
 
     span_d = 1 + (dep > 0).astype(jnp.int32) + (dep < n_dep - 1).astype(jnp.int32)
     span_h = 1 + (hgt > 0).astype(jnp.int32) + (hgt < n_hgt - 1).astype(jnp.int32)
@@ -177,23 +236,7 @@
 
     halo(v_copy, 1, "start")
 
-    for d in (0, 1):
-        for h in (0, 1, 10, 11):
-            C[d, h] = jnp.zeros((128, W), BF)
-        tmp[...] = cot[:, d].astype(F32).reshape(1024, W)
-
-        @pl.loop(0, 8)
-        def _(h):
-            C[d, 2 + h] = tmp[pl.ds(h, 128, stride=8), :].astype(BF)
-
-    for a in range(3):
-        for b in range(3):
-            for c in range(3):
-                WB[a * 192 + c * 64 : a * 192 + c * 64 + 64, (2 - b) * 128 : (3 - b) * 128] = k2t[
-                    9 * a + 3 * b + c
-                ]
-
-    @pl.loop(0, 10)
+    @pl.loop(0, 10, unroll=5)
     def _(h):
         t = dot(WB[...], pair(C, 0, h, 384))
         sums = []
@@ -215,13 +258,14 @@
 
     halo(b_copy, 1, "start")
 
+    loads[3].wait()
     for c in range(3):
         stack = [k1t[3 * t + c].astype(F32) for t in range(9)]
         W1[c * 64 : c * 64 + 64, :] = jnp.concatenate(stack, axis=0).T.astype(BF)
 
     halo(v_copy, -1, "wait_recv")
 
-    @pl.loop(0, 10)
+    @pl.loop(0, 10, unroll=5)
     def _(h):
         ok_h = ((h > 0) | (hgt > 0)) & ((h < 9) | (hgt < n_hgt - 1))
         for d in (0, 2):
@@ -230,7 +274,7 @@
             for e in (0, 1):
                 part = [t[c * 64 : c * 64 + 64, e * W : e * W + W] for c in range(3)]
                 pre = shifted(part[0], 1) + part[1] + shifted(part[2], -1)
-                sigma = 1.0 / (1.0 + jnp.exp(-pre))
+                sigma = 0.5 * jnp.tanh(0.5 * pre) + 0.5
                 ok = ok_h
                 if d + e == 0:
                     ok = ok & (dep > 0)
@@ -244,9 +288,13 @@
                     DS[d + e - 1, h] = sigma * (1.0 + pre * (1.0 - sigma))
 
     def keep(owner, unit, value):
-        value = value.reshape(n_z, rows, W)
-        G[owner, :, unit] = value
-        GB[owner, :, unit] = value.astype(BF)
+        if unit < 4:
+            GA[owner, unit] = value
+            GA16[owner, unit] = value.astype(BF)
+        else:
+            value = value.reshape(n_z, rows, W)
+            GB[owner, :, unit - 4] = value
+            GB16[owner, :, unit - 4] = value.astype(BF)
 
     upstream = [C[d, 2 + h] for h in range(8) for d in (0, 1)]
     upstream = jnp.concatenate(upstream, axis=1)
@@ -263,19 +311,120 @@
     keep(1, 3, jnp.concatenate([lasts[0, 2], lasts[1, 2]], axis=1))
     keep(1, 4, jnp.concatenate([lasts[2, 2], jnp.zeros((128, 64), F32)], axis=1))
 
+    def remote(src, dst, send, recv, peer):
+        return pltpu.make_async_remote_copy(
+            src_ref=src,
+            dst_ref=dst,
+            send_sem=send,
+            recv_sem=recv,
+            device_id=peer,
+            device_id_type=MESH,
+        )
+
+    ca = remote(GA16.at[1 - core], RCA, ca_send, ca_recv, partner)
+    cb = remote(GB16.at[1 - core], RCB, cb_send, cb_recv, partner)
+    ya = [remote(YSA.at[(y + m) % n_y], RYA.at[m], ya_send.at[m], ya_recv.at[m], y_peer(m)) for m in range(1, n_y)]
+    za = [remote(ZSA.at[(z + m) % n_z], RZA.at[m], za_send.at[m], za_recv.at[m], z_peer(m)) for m in range(1, n_z)]
+    zb = [remote(ZSB.at[(z + m) % n_z], RZB.at[m], zb_send.at[m], zb_recv.at[m], z_peer(m)) for m in range(1, n_z)]
+
+    def x_copies(buf, send, recv, arriving):
+        return [
+            remote(
+                buf.at[dep],
+                buf.at[(dep + n_dep - m) % n_dep if arriving else dep],
+                send.at[m],
+                recv.at[m],
+                x_peer(m),
+            )
+            for m in range(1, n_dep)
+        ]
+
+    def yb_copies(arriving):
+        return [
+            remote(
+                YSB.at[(y + m) % 2],
+                RYB.at[(y + n_y - m) % n_y if arriving else y],
+                yb_send.at[m],
+                yb_recv.at[m],
+                y_peer(m),
+            )
+            for m in range(1, n_y)
+        ]
+
+    def fa_copies(arriving):
+        copies = []
+        for m in range(1, n_y):
+            for far in (0, 1):
+                from_core = (1 - core if far else core) if arriving else core
+                from_y = (y + n_y - m) % n_y if arriving else y
+                to_yl = yl if arriving else (y + m) % 2
+                copies.append(
+                    remote(
+                        FA.at[core, y, (y + m) % 2],
+                        FA.at[from_core, from_y, to_yl],
+                        fa_send.at[2 * m + far],
+                        fa_recv.at[2 * m + far],
+                        y_far(m) if far else y_peer(m),
+                    )
+                )
+        copies.append(
+            remote(
+                FA.at[core, y, yl],
+                FA.at[1 - core if arriving else core, y, yl],
+                fa_send.at[0],
+                fa_recv.at[0],
+                partner,
+            )
+        )
+        return copies
+
+    def start(copies):
+        for copy in copies:
+            copy.start()
+
+    def wait(copies):
+        for copy in copies:
+            copy.wait()
+
+    def z_first():
+        cb.wait_recv()
+
+        @pl.loop(0, n_z, unroll=4)
+        def _(j):
+            ZSB[j] = (GB[core, j] + RCB[j].astype(F32)).astype(BF)
+
+        start(zb)
+
+    ca.start()
+
+    @pl.when(core == 1)
+    def _():
+        cb.start()
+
     halo(b_copy, -1, "wait_recv")
 
     for d, a in ((0, 1), (1, -1)):
         for h, b in ((0, 1), (7, -1)):
             BO[d, 1 + h] += RBH[(b + 1) // 2, d].astype(F32) + RBD[(a + 1) + (b + 1) // 2].astype(F32)
 
-    @pl.loop(0, 8)
+    @pl.loop(0, 8, unroll=4)
     def _(h):
         for d, a in ((0, 1), (1, -1)):
             back = BO[d, 1 + h] + RBX[(a + 1) // 2, h].astype(F32)
             delta = back * DS[d, 1 + h]
             for c in range(3):
                 D3[2 * h + d, c * 64 : c * 64 + 64] = shifted(delta, c - 1).astype(BF)
+
+    ca.wait()
+    for j in range(n_y):
+        for u in range(4 // n_y):
+            unit = j * (4 // n_y) + u
+            YSA[j, u] = (GA[core, unit] + RCA[unit].astype(F32)).astype(BF)
+    start(ya)
+
+    @pl.when(core == 0)
+    def _():
+        z_first()
 
     upstream = jnp.concatenate([D3[r] for r in range(16)], axis=1)
     field = [
@@ -294,43 +443,26 @@
     blocks.append(jnp.zeros((64, W), F32))
     for m in range(4):
         two = [blocks[2 * m + e].reshape(n_z, rows // 2, W) for e in (0, 1)]
-        value = jnp.concatenate(two, axis=1)
-        G[1, :, 5 + m] = value
-        GB[1, :, 5 + m] = value.astype(BF)
-
-    c_copy = pltpu.make_async_remote_copy(
-        src_ref=GB.at[1 - core],
-        dst_ref=RC,
-        send_sem=c_send,
-        recv_sem=c_recv,
-        device_id=partner,
-        device_id_type=MESH,
-    )
-    c_copy.start()
+        part = [two[e][:, f * (rows // 4) : (f + 1) * (rows // 4)] for f in (0, 1) for e in (0, 1)]
+        value = jnp.concatenate(part, axis=1)
+        GB[1, :, 1 + m] = value
+        GB16[1, :, 1 + m] = value.astype(BF)
+
+    @pl.when(core == 0)
+    def _():
+        cb.start()
+
     for c in range(3):
         stack = [k2t[3 * t + c].astype(F32) for t in range(9)]
         W2[c * 128 : c * 128 + 128, :] = jnp.concatenate(stack, axis=0).T.astype(BF)
-    c_copy.wait()
-
-    @pl.loop(0, n_z)
-    def _(j):
-        ZS[j] = (G[core, j] + RC[j].astype(F32)).astype(BF)
-
-    def z_copy(m):
-        return pltpu.make_async_remote_copy(
-            src_ref=ZS.at[(z + m) % n_z],
-            dst_ref=RZ.at[m],
-            send_sem=z_send.at[m],
-            recv_sem=z_recv.at[m],
-            device_id=z_peer(m),
-            device_id_type=MESH,
-        )
-
-    for m in range(1, n_z):
-        z_copy(m).start()
-
-    @pl.loop(0, 8)
-    def _(h):
+
+    @pl.when(core == 1)
+    def _():
+        z_first()
+
+    cb.wait_send()
+
+    def features(h):
         x = jnp.concatenate([pair(H, a, h, 192) for a in range(3)], axis=0)
         t = dot(W2[...], x)
         for d in (0, 1):
@@ -338,102 +470,80 @@
             total = shifted(part[0], 1) + part[1] + shifted(part[2], -1)
             FO[d, pl.ds(h, 128, stride=8), :] = total
 
+    pl.loop(0, 4, unroll=4)(features)
+
+    wait(ya)
+    per = 4 // n_y
+    for u in range(per):
+        total = GA[core, y * per + u] + RCA[y * per + u].astype(F32)
+        for m in range(1, n_y):
+            total = total + RYA[m, u].astype(F32)
+        total = total.reshape(n_z, rows, W)
+        TA[:, u] = total
+        ZSA[:, u] = total.astype(BF)
+    start(za)
+
+    pl.loop(4, 8, unroll=4)(features)
     for d in (0, 1):
         feat[:, d] = FO[d].reshape(128, 8, W).astype(BF)
 
+    half = rows // 2
+    wait(zb)
+    total = GB[core, z] + RCB[z].astype(F32)
     for m in range(1, n_z):
-        z_copy(m).wait()
-    total = G[core, z] + RC[z].astype(F32)
+        total = total + RZB[m].astype(F32)
+    for e in (0, 1):
+        YSB[e] = total[:, e * half : (e + 1) * half].astype(BF)
+    RYB[y] = YSB[yl]
+    start(yb_copies(False))
+
+    wait(za)
+    total = TA[z]
     for m in range(1, n_z):
-        total = total + RZ[m].astype(F32)
-    RY[y] = total.astype(BF)
-
-    def y_copy(m):
-        return pltpu.make_async_remote_copy(
-            src_ref=RY.at[y],
-            dst_ref=RY.at[y],
-            send_sem=y_send.at[m],
-            recv_sem=y_recv.at[m],
-            device_id=y_peer(m),
-            device_id_type=MESH,
-        )
-
-    def y_wait(m):
-        other = (y + n_y - m) % n_y
-        return pltpu.make_async_remote_copy(
-            src_ref=RY.at[y],
-            dst_ref=RY.at[other],
-            send_sem=y_send.at[m],
-            recv_sem=y_recv.at[m],
-            device_id=y_peer(m),
-            device_id_type=MESH,
-        )
-
+        total = total + RZA[m].astype(F32)
+    RXA[dep] = total.astype(BF)
+    start(x_copies(RXA, xa_send, xa_recv, False))
+
+    wait(yb_copies(True))
+    total = RYB[0].astype(F32)
     for m in range(1, n_y):
-        y_copy(m).start()
-    for m in range(1, n_y):
-        y_wait(m).wait()
-    total = RY[0].astype(F32)
-    for m in range(1, n_y):
-        total = total + RY[m].astype(F32)
-    RX[dep] = total.astype(BF)
-
-    def x_copy(m):
-        return pltpu.make_async_remote_copy(
-            src_ref=RX.at[dep],
-            dst_ref=RX.at[dep],
-            send_sem=x_send.at[m],
-            recv_sem=x_recv.at[m],
-            device_id=x_peer(m),
-            device_id_type=MESH,
-        )
-
-    def x_wait(m):
-        other = (dep + n_dep - m) % n_dep
-        return pltpu.make_async_remote_copy(
-            src_ref=RX.at[dep],
-            dst_ref=RX.at[other],
-            send_sem=x_send.at[m],
-            recv_sem=x_recv.at[m],
-            device_id=x_peer(m),
-            device_id_type=MESH,
-        )
-
+        total = total + RYB[m].astype(F32)
+    RXB[dep] = total.astype(BF)
+    start(x_copies(RXB, xb_send, xb_recv, False))
+
+    wait(x_copies(RXA, xa_send, xa_recv, True))
+    total = RXA[0].astype(F32)
     for m in range(1, n_dep):
-        x_copy(m).start()
+        total = total + RXA[m].astype(F32)
+    for e in (0, 1):
+        FA[core, y, e] = total[:, e * half : (e + 1) * half]
+    start(fa_copies(False))
+
+    wait(x_copies(RXB, xb_send, xb_recv, True))
+    total = RXB[0].astype(F32)
     for m in range(1, n_dep):
-        x_wait(m).wait()
-    total = RX[0].astype(F32)
-    for m in range(1, n_dep):
-        total = total + RX[m].astype(F32)
-    FS[core] = total
-
-    def f_copy(slot):
-        return pltpu.make_async_remote_copy(
-            src_ref=FS.at[core],
-            dst_ref=FS.at[slot],
-            send_sem=f_send,
-            recv_sem=f_recv,
-            device_id=partner,
-            device_id_type=MESH,
-        )
-
-    f_copy(core).start()
-    f_copy(1 - core).wait()
-
-    half = rows // 2
+        total = total + RXB[m].astype(F32)
+    FB[core] = total
+    remote(FB.at[core], FB.at[core], fb_send, fb_recv, partner).start()
+    wait(fa_copies(True))
+    remote(FB.at[core], FB.at[1 - core], fb_send, fb_recv, partner).wait()
+
+    def unit_of(owner, unit):
+        if unit < 4:
+            return FA[owner, unit // per, yl, unit % per]
+        return FB[owner, unit - 4]
+
     for t in range(9):
-        got = FS[0, t, pl.ds(pl.multiple_of(yl * half, half), half), :]
+        got = unit_of(0, t)
         g2_out[3 * t] = got[:, :64]
         g2_out[3 * t + 1] = got[:, 64:]
     taps = [(a, b) for a in range(3) for b in (0, 1)] + [(0, 2), (1, 2), (2, 2)]
     for n, (a, b) in enumerate(taps):
-        got = FS[1, n // 2, pl.ds(pl.multiple_of(yl * half, half), half), :]
+        got = unit_of(1, n // 2)
         g2_out[9 * a + 3 * b + 2] = got[:, (n % 2) * 64 : (n % 2) * 64 + 64]
     own = half // 2
     for block in range(7):
-        both = FS[1, 5 + block // 2, (block % 2) * half : (block % 2) * half + half, :]
-        got = jnp.where(yl == 0, both[:own], both[own:])
+        got = FB[1, 1 + block // 2, (block % 2) * own : (block % 2) * own + own, :]
         for n in range(4 if block < 6 else 3):
             lanes = got[:, n * 32 : n * 32 + 32]
             if block < 6:
@@ -447,7 +557,7 @@
 
 def per_device(sizes, volume, kernel_first, kernel_second, cotangent):
     n_z, n_y, n_dep, n_hgt = sizes
-    rows = 128 // n_z
+    rows, per = 128 // n_z, 4 // n_y
     vmem = pl.BlockSpec(memory_space=pltpu.VMEM)
     dma = pltpu.SemaphoreType.DMA
     features, grad_first, grad_second = pl.pallas_call(
@@ -457,9 +567,13 @@
             jax.ShapeDtypeStruct((27, rows // 4, 32), F32),
             jax.ShapeDtypeStruct((27, rows // 2, 64), F32),
         ),
-        in_specs=[vmem] * 4,
+        in_specs=[pl.BlockSpec(memory_space=pltpu.HBM)] * 4,
         out_specs=(vmem, vmem, vmem),
         scratch_shapes=[
+            pltpu.VMEM((32, 2, 8, W), BF),
+            pltpu.VMEM((27, 32, 64), BF),
+            pltpu.VMEM((27, 64, 128), BF),
+            pltpu.VMEM((128, 2, 8, W), BF),
             pltpu.VMEM((6, 12, 32, W), BF),
             pltpu.VMEM((2, 12, 128, W), BF),
             pltpu.VMEM((1024, W), F32),
@@ -475,19 +589,41 @@
             pltpu.VMEM((4, 10, 192, W), BF),
             pltpu.VMEM((2, 10, 64, W), F32),
             pltpu.VMEM((16, 192, W), BF),
-            pltpu.VMEM((2, n_z, 9, rows, W), F32),
-            pltpu.VMEM((2, n_z, 9, rows, W), BF),
-            pltpu.VMEM((n_z, 9, rows, W), BF),
-            pltpu.VMEM((n_z, 9, rows, W), BF),
-            pltpu.VMEM((n_z, 9, rows, W), BF),
-            pltpu.VMEM((n_y, 9, rows, W), BF),
-            pltpu.VMEM((n_dep, 9, rows, W), BF),
-            pltpu.VMEM((2, 9, rows, W), F32),
+            pltpu.VMEM((2, 4, 128, W), F32),
+            pltpu.VMEM((2, 4, 128, W), BF),
+            pltpu.VMEM((4, 128, W), BF),
+            pltpu.VMEM((n_y, per, 128, W), BF),
+            pltpu.VMEM((n_y, per, 128, W), BF),
+            pltpu.VMEM((n_z, per, rows, W), F32),
+            pltpu.VMEM((n_z, per, rows, W), BF),
+            pltpu.VMEM((n_z, per, rows, W), BF),
+            pltpu.VMEM((n_dep, per, rows, W), BF),
+            pltpu.VMEM((2, n_y, 2, per, rows // 2, W), F32),
+            pltpu.VMEM((2, n_z, 5, rows, W), F32),
+            pltpu.VMEM((2, n_z, 5, rows, W), BF),
+            pltpu.VMEM((n_z, 5, rows, W), BF),
+            pltpu.VMEM((n_z, 5, rows, W), BF),
+            pltpu.VMEM((n_z, 5, rows, W), BF),
+            pltpu.VMEM((2, 5, rows // 2, W), BF),
+            pltpu.VMEM((n_y, 5, rows // 2, W), BF),
+            pltpu.VMEM((n_dep, 5, rows // 2, W), BF),
+            pltpu.VMEM((2, 5, rows // 2, W), F32),
             pltpu.VMEM((2, 1024, W), F32),
+            dma((4,)),
             dma((8,)),
             dma((8,)),
             dma((8,)),
             dma((8,)),
+            dma,
+            dma,
+            dma((n_y,)),
+            dma((n_y,)),
+            dma((n_z,)),
+            dma((n_z,)),
+            dma((n_dep,)),
+            dma((n_dep,)),
+            dma((2 * n_y,)),
+            dma((2 * n_y,)),
             dma,
             dma,
             dma((n_z,)),
@@ -500,7 +636,7 @@
             dma,
         ],
         compiler_params=pltpu.CompilerParams(
-            collective_id=0, has_side_effects=True, vmem_limit_bytes=50 * 1024 * 1024
+            collective_id=0, has_side_effects=True, vmem_limit_bytes=40 * 1024 * 1024
         ),
     )(
         volume[0],

time: 53.9 us -> 47.7 us (0.88)
  Pallas kernels: 47.1 us -> 40.9 us
    pallas_call x1, Pallas kernels: 47.1 us -> 40.9 us  [per_device(): pl.pallas_call(functools.partial(kernel, sizes), out_shape=(jax.ShapeDtyp...]
where the time goes in v2:
time: 47.7 us; the launch traced here: 47.5 us
  Pallas kernels  40.9 us (86%)
  local copies, waits for them, and re-layouts  5.95 us (12%)
  between operations  0.65 us (1%)
    pallas_call x1, Pallas kernels, per_device(): pl.pallas_call(functools.partial(kernel, sizes), out_shape=(jax.ShapeDtyp...  40.9 us
    unnamed x11, local copies, waits for them, and re-layouts  5.95 us

profile of v2, /device:TPU:1, one launch (start us, length us, event | category | flops | bytes accessed | tf_op | source)
XLA Modules:
  0.0 47.5 jit_solution(7621765673262440597)
XLA Ops:
  0.6 0.0 copy-start
  0.6 1.0 %copy-done = bf16[1,128,2,8,128]{4,3,2,1,0:T(8,128)(2,1)S(1)} copy-done((bf16[1,128,2,8,128]{4,3,2,1,0:T(8,128)(2,1)S(1)}, bf16[1,128,2,8,128]{4,3,2,1,0:T(8,128)(2,1)}, u32[]{:S(2)}) %copy-start) | copy-done | bytes 524312
  1.7 0.0 copy-start.1
  1.7 1.0 %copy-done.1 = bf16[27,128,64]{1,2,0:T(8,128)(2,1)S(1)} copy-done((bf16[27,128,64]{1,2,0:T(8,128)(2,1)S(1)}, bf16[27,128,64]{1,2,0:T(8,128)(2,1)}, u32[]{:S(2)}) %copy-start.1) | copy-done | bytes 442392
  2.7 0.0 copy-start.2
  2.7 0.9 %copy-done.2 = bf16[27,64,32]{1,2,0:T(8,128)(2,1)S(1)} copy-done((bf16[27,64,32]{1,2,0:T(8,128)(2,1)S(1)}, bf16[27,64,32]{1,2,0:T(8,128)(2,1)}, u32[]{:S(2)}) %copy-start.2) | copy-done | bytes 110616
  3.6 0.0 copy-start.3
  3.6 0.9 %copy-done.3 = bf16[1,32,2,8,128]{4,3,2,1,0:T(8,128)(2,1)S(1)} copy-done((bf16[1,32,2,8,128]{4,3,2,1,0:T(8,128)(2,1)S(1)}, bf16[1,32,2,8,128]{4,3,2,1,0:T(8,128)(2,1)}, u32[]{:S(2)}) %copy-start.3) | copy-done | bytes 131096
  4.5 40.9 %shard_map.67 = (bf16[128,2,8,128]{3,2,1,0:T(8,128)(2,1)S(1)}, f32[27,4,32]{2,1,0:T(4,128)S(1)}, f32[27,8,64]{2,1,0:T(8,128)S(1)}) custom-call(bf16[32,2,8,128]{3,2,1,0:T(8,128)(2,1)S(1)} %bitcast.9, bf16[27,32,64]{2,1,0:T(8,128)(2,1)S(1)} %bitcast.8, bf16[27,64,128]{2,1,0:T(8,128)(2,1)S(1)} %bitcast.7, bf16[128,2,8,128]{3,2,1,0:T(8,128)(2,1)S(1)} %bitcast.5), custom_call_target="tpu_custom_call" | custom-call | tf_op jit(solution)/shard_map/pallas_call | solution.py:563
  45.4 0.8 %copy.10 = bf16[1,128,2,8,128]{4,3,2,1,0:T(8,128)(2,1)} copy(bf16[1,128,2,8,128]{4,3,2,1,0:T(8,128)(2,1)S(1)} %bitcast.6) | data formatting | bytes 1048576
  46.2 0.6 %copy.11 = f32[27,4,32]{2,1,0:T(4,128)} copy(f32[27,4,32]{2,1,0:T(4,128)S(1)} %get-tuple-element.13) | data formatting | bytes 27648
  46.8 0.6 %copy.12 = f32[27,8,64]{2,1,0:T(8,128)} copy(f32[27,8,64]{2,1,0:T(8,128)S(1)} %get-tuple-element.14) | data formatting | bytes 110592
Async XLA Ops:
  0.6 1.0 %copy-start = (bf16[1,128,2,8,128]{4,3,2,1,0:T(8,128)(2,1)S(1)}, bf16[1,128,2,8,128]{4,3,2,1,0:T(8,128)(2,1)}, u32[]{:S(2)}) copy-start(bf16[1,128,2,8,128]{4,3,2,1,0:T(8,128)(2,1)} %param.7) | copy-start | bytes 1572868
  1.7 1.0 %copy-start.1 = (bf16[27,128,64]{1,2,0:T(8,128)(2,1)S(1)}, bf16[27,128,64]{1,2,0:T(8,128)(2,1)}, u32[]{:S(2)}) copy-start(bf16[27,128,64]{1,2,0:T(8,128)(2,1)} %param.6) | copy-start | bytes 1327108
  2.7 0.9 %copy-start.2 = (bf16[27,64,32]{1,2,0:T(8,128)(2,1)S(1)}, bf16[27,64,32]{1,2,0:T(8,128)(2,1)}, u32[]{:S(2)}) copy-start(bf16[27,64,32]{1,2,0:T(8,128)(2,1)} %param.5) | copy-start | bytes 331780
  3.6 0.9 %copy-start.3 = (bf16[1,32,2,8,128]{4,3,2,1,0:T(8,128)(2,1)S(1)}, bf16[1,32,2,8,128]{4,3,2,1,0:T(8,128)(2,1)}, u32[]{:S(2)}) copy-start(bf16[1,32,2,8,128]{4,3,2,1,0:T(8,128)(2,1)} %param.4) | copy-start | bytes 393220

commit v3 on v2

--- a/solution.py
+++ b/solution.py
@@ -103,8 +103,6 @@
     yb_recv,
     xb_send,
     xb_recv,
-    fb_send,
-    fb_recv,
 ):
     n_z, n_y, n_dep, n_hgt = sizes
     rows = 128 // n_z
@@ -130,6 +128,9 @@
     def y_far(m):
         other = (y + m) % n_y
         return (z * 2 + other % 2, dep, (other // 2) * 2 + 1 - core)
+
+    def x_far(m):
+        return (dp, (dep + m) % n_dep, hgt + 1 - 2 * core)
 
     partner = (dp, dep, hgt + 1 - 2 * core)
 
@@ -142,11 +143,6 @@
     for load in loads:
         load.start()
 
-    V[...] = jnp.zeros_like(V)
-    RBX[...] = jnp.zeros_like(RBX)
-    RBH[...] = jnp.zeros_like(RBH)
-    RBD[...] = jnp.zeros_like(RBD)
-
     barrier = pltpu.get_barrier_semaphore()
     for direction in DIRS:
 
@@ -164,8 +160,25 @@
     peers += [y_peer(m) for m in range(1, n_y)]
     peers += [y_far(m) for m in range(1, n_y)]
     peers += [x_peer(m) for m in range(1, n_dep)]
+    peers += [x_far(m) for m in range(1, n_dep)]
     for peer in peers:
         pl.semaphore_signal(barrier, inc=1, device_id=peer, device_id_type=MESH)
+
+    for k, (a, b) in enumerate(DIRS):
+        rows_d = {0: (2, 4), 1: (0, 2), -1: (4, 6)}[a]
+        rows_h = {0: (2, 10), 1: (0, 2), -1: (10, 12)}[b]
+
+        @pl.when(jnp.logical_not(there((a, b), -1)))
+        def _():
+            block = V.at[rows_d[0] : rows_d[1], rows_h[0] : rows_h[1]]
+            block[...] = jnp.zeros(block.shape, BF)
+            if a == 0:
+                part = RBH.at[(b + 1) // 2]
+            elif b == 0:
+                part = RBX.at[(a + 1) // 2]
+            else:
+                part = RBD.at[(a + 1) + (b + 1) // 2]
+            part[...] = jnp.zeros(part.shape, BF)
 
     loads[0].wait()
     for d in (0, 1):
@@ -195,18 +208,28 @@
     span_h = 1 + (hgt > 0).astype(jnp.int32) + (hgt < n_hgt - 1).astype(jnp.int32)
     pl.semaphore_wait(barrier, span_d * span_h - 1 + len(peers))
 
-    def v_copy(k):
+    def v_copy(k, far):
         a, b = DIRS[k]
-        to_d = {0: (2, 4), 1: (0, 2), -1: (4, 6)}[a]
         from_h, to_h = {0: ((2, 10), (2, 10)), 1: ((8, 10), (0, 2)), -1: ((2, 4), (10, 12))}[b]
+        if a == 0:
+            src, dst = V.at[2:4, from_h[0] : from_h[1]], V.at[2:4, to_h[0] : to_h[1]]
+        else:
+            plane = {(1, 0): (3, 1), (1, 1): (2, 0), (-1, 0): (2, 4), (-1, 1): (3, 5)}[a, far]
+            src, dst = V.at[plane[0], from_h[0] : from_h[1]], V.at[plane[1], to_h[0] : to_h[1]]
         return pltpu.make_async_remote_copy(
-            src_ref=V.at[2:4, from_h[0] : from_h[1]],
-            dst_ref=V.at[to_d[0] : to_d[1], to_h[0] : to_h[1]],
-            send_sem=v_send.at[k],
-            recv_sem=v_recv.at[k],
+            src_ref=src,
+            dst_ref=dst,
+            send_sem=v_send.at[far, k],
+            recv_sem=v_recv.at[far, k],
             device_id=(dp, dep + a, hgt + b),
             device_id_type=MESH,
         )
+
+    def near(k):
+        return v_copy(k, 0)
+
+    def far(k):
+        return v_copy(k, 1) if DIRS[k][0] != 0 else None
 
     def b_copy(k):
         a, b = DIRS[k]
@@ -232,9 +255,12 @@
 
             @pl.when(there(direction, sign))
             def _():
-                getattr(copy(k), what)()
-
-    halo(v_copy, 1, "start")
+                one = copy(k)
+                if one is not None:
+                    getattr(one, what)()
+
+    halo(near, 1, "start")
+    halo(far, 1, "start")
 
     @pl.loop(0, 10, unroll=5)
     def _(h):
@@ -263,29 +289,29 @@
         stack = [k1t[3 * t + c].astype(F32) for t in range(9)]
         W1[c * 64 : c * 64 + 64, :] = jnp.concatenate(stack, axis=0).T.astype(BF)
 
-    halo(v_copy, -1, "wait_recv")
-
-    @pl.loop(0, 10, unroll=5)
-    def _(h):
-        ok_h = ((h > 0) | (hgt > 0)) & ((h < 9) | (hgt < n_hgt - 1))
-        for d in (0, 2):
-            x = jnp.concatenate([pair(V, d + a, h, 96) for a in range(3)], axis=0)
-            t = dot(W1[...], x)
-            for e in (0, 1):
+    halo(near, -1, "wait_recv")
+
+    def hidden(planes):
+        def body(h):
+            ok_h = ((h > 0) | (hgt > 0)) & ((h < 9) | (hgt < n_hgt - 1))
+            x = [
+                jnp.concatenate([V[d + a, pl.ds(h, 3)].reshape(96, W) for d in planes], axis=1)
+                for a in range(3)
+            ]
+            t = dot(W1[...], jnp.concatenate(x, axis=0))
+            for e, d in enumerate(planes):
                 part = [t[c * 64 : c * 64 + 64, e * W : e * W + W] for c in range(3)]
                 pre = shifted(part[0], 1) + part[1] + shifted(part[2], -1)
                 sigma = 0.5 * jnp.tanh(0.5 * pre) + 0.5
-                ok = ok_h
-                if d + e == 0:
-                    ok = ok & (dep > 0)
-                elif d + e == 3:
-                    ok = ok & (dep < n_dep - 1)
+                ok = {0: ok_h & (dep > 0), 3: ok_h & (dep < n_dep - 1)}.get(d, ok_h)
                 hid = pre * sigma * ok.astype(F32)
-                H[d + e, h] = hid.astype(BF)
+                H[d, h] = hid.astype(BF)
                 for c in range(3):
-                    H3[d + e, h, c * 64 : c * 64 + 64] = shifted(hid, 1 - c).astype(BF)
-                if d + e in (1, 2):
-                    DS[d + e - 1, h] = sigma * (1.0 + pre * (1.0 - sigma))
+                    H3[d, h, c * 64 : c * 64 + 64] = shifted(hid, 1 - c).astype(BF)
+                if d in (1, 2):
+                    DS[d - 1, h] = sigma * (1.0 + pre * (1.0 - sigma))
+
+        pl.loop(0, 10, unroll=5)(body)
 
     def keep(owner, unit, value):
         if unit < 4:
@@ -296,10 +322,11 @@
             GB[owner, :, unit - 4] = value
             GB16[owner, :, unit - 4] = value.astype(BF)
 
-    upstream = [C[d, 2 + h] for h in range(8) for d in (0, 1)]
-    upstream = jnp.concatenate(upstream, axis=1)
     lasts = {}
-    for a in range(3):
+
+    def second(a):
+        upstream = [C[d, 2 + h] for h in range(8) for d in (0, 1)]
+        upstream = jnp.concatenate(upstream, axis=1)
         for b in range(3):
             field = [H3[d + a, h + b] for h in range(8) for d in (0, 1)]
             part = lax.dot_general(
@@ -308,7 +335,14 @@
             keep(0, 3 * a + b, part[:, :128])
             lasts[a, b] = part[:, 128:192]
         keep(1, a, jnp.concatenate([lasts[a, 0], lasts[a, 1]], axis=1))
+
+    hidden((1, 2))
+    second(1)
+    halo(far, -1, "wait_recv")
+    hidden((0, 3))
+    second(0)
     keep(1, 3, jnp.concatenate([lasts[0, 2], lasts[1, 2]], axis=1))
+    second(2)
     keep(1, 4, jnp.concatenate([lasts[2, 2], jnp.zeros((128, 64), F32)], axis=1))
 
     def remote(src, dst, send, recv, peer):
@@ -327,17 +361,35 @@
     za = [remote(ZSA.at[(z + m) % n_z], RZA.at[m], za_send.at[m], za_recv.at[m], z_peer(m)) for m in range(1, n_z)]
     zb = [remote(ZSB.at[(z + m) % n_z], RZB.at[m], zb_send.at[m], zb_recv.at[m], z_peer(m)) for m in range(1, n_z)]
 
-    def x_copies(buf, send, recv, arriving):
+    def xa_copies(arriving):
         return [
             remote(
-                buf.at[dep],
-                buf.at[(dep + n_dep - m) % n_dep if arriving else dep],
-                send.at[m],
-                recv.at[m],
+                RXA.at[dep],
+                RXA.at[(dep + n_dep - m) % n_dep if arriving else dep],
+                xa_send.at[m],
+                xa_recv.at[m],
                 x_peer(m),
             )
             for m in range(1, n_dep)
         ]
+
+    def xb_copies(arriving):
+        copies = []
+        for m in range(n_dep):
+            for other in (0, 1):
+                if m + other > 0:
+                    slot = (dep + n_dep - m) % n_dep if arriving else dep
+                    half = 1 - core if arriving and other else core
+                    copies.append(
+                        remote(
+                            RXB.at[core, dep],
+                            RXB.at[half, slot],
+                            xb_send.at[2 * m + other],
+                            xb_recv.at[2 * m + other],
+                            (x_far if other else x_peer)(m) if m else partner,
+                        )
+                    )
+        return copies
 
     def yb_copies(arriving):
         return [
@@ -382,9 +434,12 @@
         for copy in copies:
             copy.start()
 
+    sent = []
+
     def wait(copies):
+        sent.extend(copies)
         for copy in copies:
-            copy.wait()
+            copy.wait_recv()
 
     def z_first():
         cb.wait_recv()
@@ -415,7 +470,7 @@
             for c in range(3):
                 D3[2 * h + d, c * 64 : c * 64 + 64] = shifted(delta, c - 1).astype(BF)
 
-    ca.wait()
+    ca.wait_recv()
     for j in range(n_y):
         for u in range(4 // n_y):
             unit = j * (4 // n_y) + u
@@ -460,8 +515,6 @@
     def _():
         z_first()
 
-    cb.wait_send()
-
     def features(h):
         x = jnp.concatenate([pair(H, a, h, 192) for a in range(3)], axis=0)
         t = dot(W2[...], x)
@@ -502,16 +555,16 @@
     for m in range(1, n_z):
         total = total + RZA[m].astype(F32)
     RXA[dep] = total.astype(BF)
-    start(x_copies(RXA, xa_send, xa_recv, False))
+    start(xa_copies(False))
 
     wait(yb_copies(True))
     total = RYB[0].astype(F32)
     for m in range(1, n_y):
         total = total + RYB[m].astype(F32)
-    RXB[dep] = total.astype(BF)
-    start(x_copies(RXB, xb_send, xb_recv, False))
-
-    wait(x_copies(RXA, xa_send, xa_recv, True))
+    RXB[core, dep] = total.astype(BF)
+    start(xb_copies(False))
+
+    wait(xa_copies(True))
     total = RXA[0].astype(F32)
     for m in range(1, n_dep):
         total = total + RXA[m].astype(F32)
@@ -519,14 +572,13 @@
         FA[core, y, e] = total[:, e * half : (e + 1) * half]
     start(fa_copies(False))
 
-    wait(x_copies(RXB, xb_send, xb_recv, True))
-    total = RXB[0].astype(F32)
-    for m in range(1, n_dep):
-        total = total + RXB[m].astype(F32)
-    FB[core] = total
-    remote(FB.at[core], FB.at[core], fb_send, fb_recv, partner).start()
+    wait(xb_copies(True))
+    for c in (0, 1):
+        total = RXB[c, 0].astype(F32)
+        for m in range(1, n_dep):
+            total = total + RXB[c, m].astype(F32)
+        FB[c] = total
     wait(fa_copies(True))
-    remote(FB.at[core], FB.at[1 - core], fb_send, fb_recv, partner).wait()
 
     def unit_of(owner, unit):
         if unit < 4:
@@ -551,8 +603,20 @@
             else:
                 g1_out[24 + n] = lanes
 
-    halo(v_copy, 1, "wait_send")
+    for copy in sent + [ca, cb]:
+        copy.wait_send()
+    halo(near, 1, "wait_send")
+    halo(far, 1, "wait_send")
     halo(b_copy, 1, "wait_send")
+
+
+def write_out(*refs):
+    sem = refs[6]
+    copies = [pltpu.make_async_copy(refs[n], refs[3 + n], sem.at[n]) for n in range(3)]
+    for copy in copies:
+        copy.start()
+    for copy in copies:
+        copy.wait()
 
 
 def per_device(sizes, volume, kernel_first, kernel_second, cotangent):
@@ -560,7 +624,7 @@
     rows, per = 128 // n_z, 4 // n_y
     vmem = pl.BlockSpec(memory_space=pltpu.VMEM)
     dma = pltpu.SemaphoreType.DMA
-    features, grad_first, grad_second = pl.pallas_call(
+    results = pl.pallas_call(
         functools.partial(kernel, sizes),
         out_shape=(
             jax.ShapeDtypeStruct((128, 2, 8, W), BF),
@@ -606,12 +670,12 @@
             pltpu.VMEM((n_z, 5, rows, W), BF),
             pltpu.VMEM((2, 5, rows // 2, W), BF),
             pltpu.VMEM((n_y, 5, rows // 2, W), BF),
-            pltpu.VMEM((n_dep, 5, rows // 2, W), BF),
+            pltpu.VMEM((2, n_dep, 5, rows // 2, W), BF),
             pltpu.VMEM((2, 5, rows // 2, W), F32),
             pltpu.VMEM((2, 1024, W), F32),
             dma((4,)),
-            dma((8,)),
-            dma((8,)),
+            dma((2, 8)),
+            dma((2, 8)),
             dma((8,)),
             dma((8,)),
             dma,
@@ -630,20 +694,31 @@
             dma((n_z,)),
             dma((n_y,)),
             dma((n_y,)),
-            dma((n_dep,)),
-            dma((n_dep,)),
-            dma,
-            dma,
+            dma((2 * n_dep,)),
+            dma((2 * n_dep,)),
         ],
         compiler_params=pltpu.CompilerParams(
             collective_id=0, has_side_effects=True, vmem_limit_bytes=40 * 1024 * 1024
         ),
     )(
-        volume[0],
-        kernel_first.swapaxes(1, 2),
-        kernel_second.swapaxes(1, 2),
-        cotangent[0],
+        *[
+            pltpu.with_memory_space_constraint(x, pltpu.HBM)
+            for x in (
+                volume[0],
+                kernel_first.swapaxes(1, 2),
+                kernel_second.swapaxes(1, 2),
+                cotangent[0],
+            )
+        ]
     )
+    features, grad_first, grad_second = pl.pallas_call(
+        write_out,
+        out_shape=tuple(jax.ShapeDtypeStruct(x.shape, x.dtype) for x in results),
+        in_specs=[vmem] * 3,
+        out_specs=(pl.BlockSpec(memory_space=pltpu.HBM),) * 3,
+        scratch_shapes=[dma((3,))],
+        compiler_params=pltpu.CompilerParams(vmem_limit_bytes=8 * 1024 * 1024),
+    )(*results)
     return features[None], grad_first, grad_second
 
 

time: 47.7 us -> 40 us (0.84)
  local copies, waits for them, and re-layouts: 5.95 us -> 0 us
  Pallas kernels: 40.9 us -> 39.2 us
    unnamed x11 -> x0, local copies, waits for them, and re-layouts: 5.95 us -> none
    pallas_call x1, Pallas kernels: 40.9 us -> 38.4 us  [per_device(): pl.pallas_call(functools.partial(kernel, sizes), out_shape=(jax.ShapeDtyp...]
    pallas_call x0 -> x1, Pallas kernels: none -> 0.86 us  [per_device(): pl.pallas_call(write_out, out_shape=tuple((jax.ShapeDtypeStruct(x.shape,...]
where the time goes in v3:
time: 40 us; the launch traced here: 39.9 us
  Pallas kernels  39.2 us (98%)
  between operations  0.64 us (2%)
    pallas_call x1, Pallas kernels, per_device(): pl.pallas_call(functools.partial(kernel, sizes), out_shape=(jax.ShapeDtyp...  38.4 us
    pallas_call x1, Pallas kernels, per_device(): pl.pallas_call(write_out, out_shape=tuple((jax.ShapeDtypeStruct(x.shape,...  0.86 us

profile of v3, /device:TPU:1, one launch (start us, length us, event | category | flops | bytes accessed | tf_op | source)
XLA Modules:
  0.0 39.9 jit_solution(15299995733788716565)
XLA Ops:
  0.6 38.4 %shard_map.67 = (bf16[128,2,8,128]{3,2,1,0:T(8,128)(2,1)S(1)}, f32[27,4,32]{2,1,0:T(4,128)S(1)}, f32[27,8,64]{2,1,0:T(8,128)S(1)}) custom-call(bf16[32,2,8,128]{3,2,1,0:T(8,128)(2,1)} %bitcast.8, bf16[27,32,64]{2,1,0:T(8,128)(2,1)} %bitcast.7, bf16[27,64,128]{2,1,0:T(8,128)(2,1)} %bitcast.6, bf16[128,2,8,128]{3,2,1,0:T(8,128)(2,1)} %bitcast.5), custom_call_target="tpu_custom_call" | custom-call | tf_op jit(solution)/shard_map/pallas_call | solution.py:627
  39.0 0.9 %shard_map.68 = (bf16[128,2,8,128]{3,2,1,0:T(8,128)(2,1)}, f32[27,4,32]{2,1,0:T(4,128)}, f32[27,8,64]{2,1,0:T(8,128)}) custom-call(bf16[128,2,8,128]{3,2,1,0:T(8,128)(2,1)S(1)} %get-tuple-element.9.refs_0_, f32[27,4,32]{2,1,0:T(4,128)S(1)} %get-tuple-element.10.refs_1_, f32[27,8,64]{2,1,0:T(8,128)S(1)} %get-tuple-element.11.refs_2_), custom_call_target="tpu_custom_call" | custom-call | tf_op jit(solution)/shard_map/pallas_call | solution.py:714

commit v4 on v3

--- a/solution.py
+++ b/solution.py
@@ -51,15 +51,12 @@
     W1,
     W2,
     WB,
-    BS,
     BO,
-    RBX,
-    RBH,
-    RBD,
     H,
     H3,
-    DS,
     D3,
+    PN,
+    P1,
     GA,
     GA16,
     RCA,
@@ -68,6 +65,7 @@
     TA,
     ZSA,
     RZA,
+    YSX,
     RXA,
     FA,
     GB,
@@ -83,8 +81,6 @@
     in_sem,
     v_send,
     v_recv,
-    b_send,
-    b_recv,
     ca_send,
     ca_recv,
     ya_send,
@@ -93,8 +89,6 @@
     za_recv,
     xa_send,
     xa_recv,
-    fa_send,
-    fa_recv,
     cb_send,
     cb_recv,
     zb_send,
@@ -125,12 +119,18 @@
     def x_peer(m):
         return (dp, (dep + m) % n_dep, hgt)
 
-    def y_far(m):
-        other = (y + m) % n_y
-        return (z * 2 + other % 2, dep, (other // 2) * 2 + 1 - core)
-
-    def x_far(m):
-        return (dp, (dep + m) % n_dep, hgt + 1 - 2 * core)
+    def plane_peer(mx, my, far):
+        other = (y + my) % n_y
+        side = 1 - core if far else core
+        return (z * 2 + other % 2, (dep + mx) % n_dep, (other // 2) * 2 + side)
+
+    plane = [
+        (mx, my, far)
+        for mx in range(n_dep)
+        for my in range(n_y)
+        for far in (0, 1)
+        if mx + my + far > 0
+    ]
 
     partner = (dp, dep, hgt + 1 - 2 * core)
 
@@ -144,23 +144,7 @@
         load.start()
 
     barrier = pltpu.get_barrier_semaphore()
-    for direction in DIRS:
-
-        @pl.when(there(direction, 1))
-        def _():
-            pl.semaphore_signal(
-                barrier,
-                inc=1,
-                device_id=(dp, dep + direction[0], hgt + direction[1]),
-                device_id_type=MESH,
-            )
-
-    peers = [partner]
-    peers += [z_peer(m) for m in range(1, n_z)]
-    peers += [y_peer(m) for m in range(1, n_y)]
-    peers += [y_far(m) for m in range(1, n_y)]
-    peers += [x_peer(m) for m in range(1, n_dep)]
-    peers += [x_far(m) for m in range(1, n_dep)]
+    peers = [plane_peer(*p) for p in plane] + [z_peer(m) for m in range(1, n_z)]
     for peer in peers:
         pl.semaphore_signal(barrier, inc=1, device_id=peer, device_id_type=MESH)
 
@@ -172,13 +156,6 @@
         def _():
             block = V.at[rows_d[0] : rows_d[1], rows_h[0] : rows_h[1]]
             block[...] = jnp.zeros(block.shape, BF)
-            if a == 0:
-                part = RBH.at[(b + 1) // 2]
-            elif b == 0:
-                part = RBX.at[(a + 1) // 2]
-            else:
-                part = RBD.at[(a + 1) + (b + 1) // 2]
-            part[...] = jnp.zeros(part.shape, BF)
 
     loads[0].wait()
     for d in (0, 1):
@@ -204,9 +181,7 @@
                     9 * a + 3 * b + c
                 ]
 
-    span_d = 1 + (dep > 0).astype(jnp.int32) + (dep < n_dep - 1).astype(jnp.int32)
-    span_h = 1 + (hgt > 0).astype(jnp.int32) + (hgt < n_hgt - 1).astype(jnp.int32)
-    pl.semaphore_wait(barrier, span_d * span_h - 1 + len(peers))
+    pl.semaphore_wait(barrier, len(peers))
 
     def v_copy(k, far):
         a, b = DIRS[k]
@@ -231,25 +206,6 @@
     def far(k):
         return v_copy(k, 1) if DIRS[k][0] != 0 else None
 
-    def b_copy(k):
-        a, b = DIRS[k]
-        d = {-1: 0, 1: 3}.get(a)
-        h = {-1: 0, 1: 9}.get(b)
-        if a == 0:
-            src, dst = BS.at[1:3, h], RBH.at[(b + 1) // 2]
-        elif b == 0:
-            src, dst = BS.at[d, 1:9], RBX.at[(a + 1) // 2]
-        else:
-            src, dst = BS.at[d, h], RBD.at[(a + 1) + (b + 1) // 2]
-        return pltpu.make_async_remote_copy(
-            src_ref=src,
-            dst_ref=dst,
-            send_sem=b_send.at[k],
-            recv_sem=b_recv.at[k],
-            device_id=(dp, dep + a, hgt + b),
-            device_id_type=MESH,
-        )
-
     def halo(copy, sign, what):
         for k, direction in enumerate(DIRS):
 
@@ -275,19 +231,19 @@
                 ]
                 halves.append(parts[0] + parts[1] + parts[2])
             sums.append(halves)
-        inner = [sums[0][1] + sums[1][0], sums[1][1] + sums[2][0]]
-        BS[0, h] = sums[0][0].astype(BF)
-        BS[3, h] = sums[2][1].astype(BF)
-        for d in (0, 1):
-            BS[1 + d, h] = inner[d].astype(BF)
-            BO[d, h] = inner[d]
-
-    halo(b_copy, 1, "start")
+        BO[0, h] = sums[0][0]
+        BO[1, h] = sums[0][1] + sums[1][0]
+        BO[2, h] = sums[1][1] + sums[2][0]
+        BO[3, h] = sums[2][1]
 
     loads[3].wait()
     for c in range(3):
         stack = [k1t[3 * t + c].astype(F32) for t in range(9)]
         W1[c * 64 : c * 64 + 64, :] = jnp.concatenate(stack, axis=0).T.astype(BF)
+
+    for c in range(3):
+        stack = [k2t[3 * t + c].astype(F32) for t in range(9)]
+        W2[c * 128 : c * 128 + 128, :] = jnp.concatenate(stack, axis=0).T.astype(BF)
 
     halo(near, -1, "wait_recv")
 
@@ -304,12 +260,13 @@
                 pre = shifted(part[0], 1) + part[1] + shifted(part[2], -1)
                 sigma = 0.5 * jnp.tanh(0.5 * pre) + 0.5
                 ok = {0: ok_h & (dep > 0), 3: ok_h & (dep < n_dep - 1)}.get(d, ok_h)
-                hid = pre * sigma * ok.astype(F32)
+                ok = ok.astype(F32)
+                hid = pre * sigma * ok
+                delta = BO[d, h] * (sigma * (1.0 + pre * (1.0 - sigma)) * ok)
                 H[d, h] = hid.astype(BF)
                 for c in range(3):
                     H3[d, h, c * 64 : c * 64 + 64] = shifted(hid, 1 - c).astype(BF)
-                if d in (1, 2):
-                    DS[d - 1, h] = sigma * (1.0 + pre * (1.0 - sigma))
+                    D3[d, h, c * 64 : c * 64 + 64] = shifted(delta, c - 1).astype(BF)
 
         pl.loop(0, 10, unroll=5)(body)
 
@@ -324,25 +281,44 @@
 
     lasts = {}
 
-    def second(a):
-        upstream = [C[d, 2 + h] for h in range(8) for d in (0, 1)]
-        upstream = jnp.concatenate(upstream, axis=1)
+    def product(left, right):
+        left, right = (jnp.concatenate(side, axis=1) for side in (left, right))
+        return lax.dot_general(left, right, NT, preferred_element_type=F32)
+
+    def second(a, b, planes):
+        return product(
+            [C[d, 2 + h] for d in planes for h in range(8)],
+            [H3[d + a, h + b] for d in planes for h in range(8)],
+        )
+
+    def keep_second(a, b, part):
+        keep(0, 3 * a + b, part[:, :128])
+        lasts[a, b] = part[:, 128:192]
+
+    def first(planes):
+        cells = [(d, h) for d in planes for h in range(10)]
+        field = [
+            jnp.concatenate([V[d + a, h : h + 3].reshape(96, W) for a in range(3)], axis=0)
+            for d, h in cells
+        ]
+        return product([D3[d, h] for d, h in cells], field)
+
+    hidden((1, 2))
+    for b in range(3):
+        keep_second(1, b, second(1, b, (0, 1)))
+    for n, (a, d) in enumerate(((0, 1), (2, 0))):
         for b in range(3):
-            field = [H3[d + a, h + b] for h in range(8) for d in (0, 1)]
-            part = lax.dot_general(
-                upstream, jnp.concatenate(field, axis=1), NT, preferred_element_type=F32
-            )
-            keep(0, 3 * a + b, part[:, :128])
-            lasts[a, b] = part[:, 128:192]
-        keep(1, a, jnp.concatenate([lasts[a, 0], lasts[a, 1]], axis=1))
-
-    hidden((1, 2))
-    second(1)
+            PN[3 * n + b] = second(a, b, (d,))
+    P1[...] = first((1, 2))
+
     halo(far, -1, "wait_recv")
     hidden((0, 3))
-    second(0)
+    for n, (a, d) in enumerate(((0, 0), (2, 1))):
+        for b in range(3):
+            keep_second(a, b, second(a, b, (d,)) + PN[3 * n + b])
+    for a in range(3):
+        keep(1, a, jnp.concatenate([lasts[a, 0], lasts[a, 1]], axis=1))
     keep(1, 3, jnp.concatenate([lasts[0, 2], lasts[1, 2]], axis=1))
-    second(2)
     keep(1, 4, jnp.concatenate([lasts[2, 2], jnp.zeros((128, 64), F32)], axis=1))
 
     def remote(src, dst, send, recv, peer):
@@ -362,16 +338,21 @@
     zb = [remote(ZSB.at[(z + m) % n_z], RZB.at[m], zb_send.at[m], zb_recv.at[m], z_peer(m)) for m in range(1, n_z)]
 
     def xa_copies(arriving):
-        return [
-            remote(
-                RXA.at[dep],
-                RXA.at[(dep + n_dep - m) % n_dep if arriving else dep],
-                xa_send.at[m],
-                xa_recv.at[m],
-                x_peer(m),
+        copies = []
+        for n, (mx, my, far) in enumerate(plane):
+            from_core = 1 - core if arriving and far else core
+            from_y = (y + n_y - my) % n_y if arriving else y
+            from_x = (dep + n_dep - mx) % n_dep if arriving else dep
+            copies.append(
+                remote(
+                    YSX.at[(y + my) % 2],
+                    RXA.at[from_core, from_y, from_x],
+                    xa_send.at[n],
+                    xa_recv.at[n],
+                    plane_peer(mx, my, far),
+                )
             )
-            for m in range(1, n_dep)
-        ]
+        return copies
 
     def xb_copies(arriving):
         copies = []
@@ -386,7 +367,7 @@
                             RXB.at[half, slot],
                             xb_send.at[2 * m + other],
                             xb_recv.at[2 * m + other],
-                            (x_far if other else x_peer)(m) if m else partner,
+                            plane_peer(m, 0, other),
                         )
                     )
         return copies
@@ -403,33 +384,6 @@
             for m in range(1, n_y)
         ]
 
-    def fa_copies(arriving):
-        copies = []
-        for m in range(1, n_y):
-            for far in (0, 1):
-                from_core = (1 - core if far else core) if arriving else core
-                from_y = (y + n_y - m) % n_y if arriving else y
-                to_yl = yl if arriving else (y + m) % 2
-                copies.append(
-                    remote(
-                        FA.at[core, y, (y + m) % 2],
-                        FA.at[from_core, from_y, to_yl],
-                        fa_send.at[2 * m + far],
-                        fa_recv.at[2 * m + far],
-                        y_far(m) if far else y_peer(m),
-                    )
-                )
-        copies.append(
-            remote(
-                FA.at[core, y, yl],
-                FA.at[1 - core if arriving else core, y, yl],
-                fa_send.at[0],
-                fa_recv.at[0],
-                partner,
-            )
-        )
-        return copies
-
     def start(copies):
         for copy in copies:
             copy.start()
@@ -441,57 +395,13 @@
         for copy in copies:
             copy.wait_recv()
 
-    def z_first():
-        cb.wait_recv()
-
-        @pl.loop(0, n_z, unroll=4)
-        def _(j):
-            ZSB[j] = (GB[core, j] + RCB[j].astype(F32)).astype(BF)
-
-        start(zb)
-
     ca.start()
 
     @pl.when(core == 1)
     def _():
         cb.start()
 
-    halo(b_copy, -1, "wait_recv")
-
-    for d, a in ((0, 1), (1, -1)):
-        for h, b in ((0, 1), (7, -1)):
-            BO[d, 1 + h] += RBH[(b + 1) // 2, d].astype(F32) + RBD[(a + 1) + (b + 1) // 2].astype(F32)
-
-    @pl.loop(0, 8, unroll=4)
-    def _(h):
-        for d, a in ((0, 1), (1, -1)):
-            back = BO[d, 1 + h] + RBX[(a + 1) // 2, h].astype(F32)
-            delta = back * DS[d, 1 + h]
-            for c in range(3):
-                D3[2 * h + d, c * 64 : c * 64 + 64] = shifted(delta, c - 1).astype(BF)
-
-    ca.wait_recv()
-    for j in range(n_y):
-        for u in range(4 // n_y):
-            unit = j * (4 // n_y) + u
-            YSA[j, u] = (GA[core, unit] + RCA[unit].astype(F32)).astype(BF)
-    start(ya)
-
-    @pl.when(core == 0)
-    def _():
-        z_first()
-
-    upstream = jnp.concatenate([D3[r] for r in range(16)], axis=1)
-    field = [
-        jnp.concatenate(
-            [V[2 + d + a - 1, 2 + h - 1 : 2 + h + 2].reshape(96, W) for a in range(3)], axis=0
-        )
-        for h in range(8)
-        for d in (0, 1)
-    ]
-    part = lax.dot_general(
-        upstream, jnp.concatenate(field, axis=1), NT, preferred_element_type=F32
-    )
+    part = first((0, 3)) + P1[...]
     blocks = [part[c * 64 : c * 64 + 64, j * W : j * W + W] for c in range(3) for j in (0, 1)]
     ends = [part[c * 64 : c * 64 + 64, 256:288] for c in range(3)]
     blocks.append(jnp.concatenate(ends + [jnp.zeros((64, 32), F32)], axis=1))
@@ -507,13 +417,19 @@
     def _():
         cb.start()
 
-    for c in range(3):
-        stack = [k2t[3 * t + c].astype(F32) for t in range(9)]
-        W2[c * 128 : c * 128 + 128, :] = jnp.concatenate(stack, axis=0).T.astype(BF)
-
-    @pl.when(core == 1)
-    def _():
-        z_first()
+    ca.wait_recv()
+    for j in range(n_y):
+        for u in range(4 // n_y):
+            unit = j * (4 // n_y) + u
+            YSA[j, u] = (GA[core, unit] + RCA[unit].astype(F32)).astype(BF)
+    start(ya)
+    cb.wait_recv()
+
+    @pl.loop(0, n_z, unroll=4)
+    def _(j):
+        ZSB[j] = (GB[core, j] + RCB[j].astype(F32)).astype(BF)
+
+    start(zb)
 
     def features(h):
         x = jnp.concatenate([pair(H, a, h, 192) for a in range(3)], axis=0)
@@ -554,7 +470,9 @@
     total = TA[z]
     for m in range(1, n_z):
         total = total + RZA[m].astype(F32)
-    RXA[dep] = total.astype(BF)
+    for e in (0, 1):
+        YSX[e] = total[:, e * half : (e + 1) * half].astype(BF)
+    RXA[core, y, dep] = YSX[yl]
     start(xa_copies(False))
 
     wait(yb_copies(True))
@@ -565,24 +483,22 @@
     start(xb_copies(False))
 
     wait(xa_copies(True))
-    total = RXA[0].astype(F32)
-    for m in range(1, n_dep):
-        total = total + RXA[m].astype(F32)
-    for e in (0, 1):
-        FA[core, y, e] = total[:, e * half : (e + 1) * half]
-    start(fa_copies(False))
-
+    for c in (0, 1):
+        for j in range(n_y):
+            total = RXA[c, j, 0].astype(F32)
+            for m in range(1, n_dep):
+                total = total + RXA[c, j, m].astype(F32)
+            FA[c, j] = total
     wait(xb_copies(True))
     for c in (0, 1):
         total = RXB[c, 0].astype(F32)
         for m in range(1, n_dep):
             total = total + RXB[c, m].astype(F32)
         FB[c] = total
-    wait(fa_copies(True))
 
     def unit_of(owner, unit):
         if unit < 4:
-            return FA[owner, unit // per, yl, unit % per]
+            return FA[owner, unit // per, unit % per]
         return FB[owner, unit - 4]
 
     for t in range(9):
@@ -607,7 +523,6 @@
         copy.wait_send()
     halo(near, 1, "wait_send")
     halo(far, 1, "wait_send")
-    halo(b_copy, 1, "wait_send")
 
 
 def write_out(*refs):
@@ -644,15 +559,12 @@
             pltpu.VMEM((192, 288), BF),
             pltpu.VMEM((384, 576), BF),
             pltpu.VMEM((576, 384), BF),
-            pltpu.VMEM((4, 10, 64, W), BF),
-            pltpu.VMEM((2, 10, 64, W), F32),
-            pltpu.VMEM((2, 8, 64, W), BF),
-            pltpu.VMEM((2, 2, 64, W), BF),
-            pltpu.VMEM((4, 64, W), BF),
+            pltpu.VMEM((4, 10, 64, W), F32),
             pltpu.VMEM((4, 10, 64, W), BF),
             pltpu.VMEM((4, 10, 192, W), BF),
-            pltpu.VMEM((2, 10, 64, W), F32),
-            pltpu.VMEM((16, 192, W), BF),
+            pltpu.VMEM((4, 10, 192, W), BF),
+            pltpu.VMEM((6, 128, 192), F32),
+            pltpu.VMEM((192, 288), F32),
             pltpu.VMEM((2, 4, 128, W), F32),
             pltpu.VMEM((2, 4, 128, W), BF),
             pltpu.VMEM((4, 128, W), BF),
@@ -661,8 +573,9 @@
             pltpu.VMEM((n_z, per, rows, W), F32),
             pltpu.VMEM((n_z, per, rows, W), BF),
             pltpu.VMEM((n_z, per, rows, W), BF),
-            pltpu.VMEM((n_dep, per, rows, W), BF),
-            pltpu.VMEM((2, n_y, 2, per, rows // 2, W), F32),
+            pltpu.VMEM((2, per, rows // 2, W), BF),
+            pltpu.VMEM((2, n_y, n_dep, per, rows // 2, W), BF),
+            pltpu.VMEM((2, n_y, per, rows // 2, W), F32),
             pltpu.VMEM((2, n_z, 5, rows, W), F32),
             pltpu.VMEM((2, n_z, 5, rows, W), BF),
             pltpu.VMEM((n_z, 5, rows, W), BF),
@@ -676,18 +589,14 @@
             dma((4,)),
             dma((2, 8)),
             dma((2, 8)),
-            dma((8,)),
-            dma((8,)),
             dma,
             dma,
             dma((n_y,)),
             dma((n_y,)),
             dma((n_z,)),
             dma((n_z,)),
-            dma((n_dep,)),
-            dma((n_dep,)),
-            dma((2 * n_y,)),
-            dma((2 * n_y,)),
+            dma((2 * n_y * n_dep,)),
+            dma((2 * n_y * n_dep,)),
             dma,
             dma,
             dma((n_z,)),

time: 40 us -> 40.2 us (level)
  no operation moved by 1% of the time
where the time goes in v4:
time: 40.2 us; the launch traced here: 40.1 us
  Pallas kernels  39.4 us (98%)
  between operations  0.64 us (2%)
    pallas_call x1, Pallas kernels, per_device(): pl.pallas_call(functools.partial(kernel, sizes), out_shape=(jax.ShapeDtyp...  38.6 us
    pallas_call x1, Pallas kernels, per_device(): pl.pallas_call(write_out, out_shape=tuple((jax.ShapeDtypeStruct(x.shape,...  0.86 us

profile of v4, /device:TPU:1, one launch (start us, length us, event | category | flops | bytes accessed | tf_op | source)
XLA Modules:
  0.0 40.1 jit_solution(16666535510130727030)
XLA Ops:
  0.6 38.6 %shard_map.67 = (bf16[128,2,8,128]{3,2,1,0:T(8,128)(2,1)S(1)}, f32[27,4,32]{2,1,0:T(4,128)S(1)}, f32[27,8,64]{2,1,0:T(8,128)S(1)}) custom-call(bf16[32,2,8,128]{3,2,1,0:T(8,128)(2,1)} %bitcast.8, bf16[27,32,64]{2,1,0:T(8,128)(2,1)} %bitcast.7, bf16[27,64,128]{2,1,0:T(8,128)(2,1)} %bitcast.6, bf16[128,2,8,128]{3,2,1,0:T(8,128)(2,1)} %bitcast.5), custom_call_target="tpu_custom_call" | custom-call | tf_op jit(solution)/shard_map/pallas_call | solution.py:542
  39.2 0.9 %shard_map.68 = (bf16[128,2,8,128]{3,2,1,0:T(8,128)(2,1)}, f32[27,4,32]{2,1,0:T(4,128)}, f32[27,8,64]{2,1,0:T(8,128)}) custom-call(bf16[128,2,8,128]{3,2,1,0:T(8,128)(2,1)S(1)} %get-tuple-element.9.refs_0_, f32[27,4,32]{2,1,0:T(4,128)S(1)} %get-tuple-element.10.refs_1_, f32[27,8,64]{2,1,0:T(8,128)S(1)} %get-tuple-element.11.refs_2_), custom_call_target="tpu_custom_call" | custom-call | tf_op jit(solution)/shard_map/pallas_call | solution.py:623

commit v5 on v4

--- a/solution.py
+++ b/solution.py
@@ -11,7 +11,7 @@
 BF = jnp.bfloat16
 F32 = jnp.float32
 W = 128
-DIRS = [(a, b) for a in (-1, 0, 1) for b in (-1, 0, 1) if (a, b) != (0, 0)]
+DIRS = [(-1, -1), (-1, 1), (1, -1), (1, 1), (-1, 0), (1, 0), (0, -1), (0, 1)]
 NT = (((1,), (1,)), ((), ()))
 
 
@@ -144,7 +144,10 @@
         load.start()
 
     barrier = pltpu.get_barrier_semaphore()
-    peers = [plane_peer(*p) for p in plane] + [z_peer(m) for m in range(1, n_z)]
+    peers = [(min(m, n_z - m), z_peer(m)) for m in range(1, n_z)]
+    for mx, my, side in plane:
+        peers.append((min(mx, n_dep - mx) + min(my, n_y - my), plane_peer(mx, my, side)))
+    peers = [peer for _, peer in sorted(peers, key=lambda entry: -entry[0])]
     for peer in peers:
         pl.semaphore_signal(barrier, inc=1, device_id=peer, device_id_type=MESH)
 
@@ -216,10 +219,8 @@
                     getattr(one, what)()
 
     halo(near, 1, "start")
-    halo(far, 1, "start")
-
-    @pl.loop(0, 10, unroll=5)
-    def _(h):
+
+    def back(h):
         t = dot(WB[...], pair(C, 0, h, 384))
         sums = []
         for a in range(3):
@@ -236,6 +237,9 @@
         BO[2, h] = sums[1][1] + sums[2][0]
         BO[3, h] = sums[2][1]
 
+    pl.loop(0, 5, unroll=5)(back)
+    halo(far, 1, "start")
+    pl.loop(5, 10, unroll=10 - 5)(back)
     loads[3].wait()
     for c in range(3):
         stack = [k1t[3 * t + c].astype(F32) for t in range(9)]

time: 40.2 us -> 39.7 us (0.988)
  Pallas kernels: 39.4 us -> 38.9 us
    pallas_call x1, Pallas kernels: 38.6 us -> 38.1 us  [per_device(): pl.pallas_call(functools.partial(kernel, sizes), out_shape=(jax.ShapeDtyp...]
where the time goes in v5:
time: 39.7 us; the launch traced here: 39.6 us
  Pallas kernels  38.9 us (98%)
  between operations  0.64 us (2%)
    pallas_call x1, Pallas kernels, per_device(): pl.pallas_call(functools.partial(kernel, sizes), out_shape=(jax.ShapeDtyp...  38.1 us
    pallas_call x1, Pallas kernels, per_device(): pl.pallas_call(write_out, out_shape=tuple((jax.ShapeDtypeStruct(x.shape,...  0.86 us

profile of v5, /device:TPU:1, one launch (start us, length us, event | category | flops | bytes accessed | tf_op | source)
XLA Modules:
  0.0 39.6 jit_solution(8556580876544731937)
XLA Ops:
  0.6 38.1 %shard_map.67 = (bf16[128,2,8,128]{3,2,1,0:T(8,128)(2,1)S(1)}, f32[27,4,32]{2,1,0:T(4,128)S(1)}, f32[27,8,64]{2,1,0:T(8,128)S(1)}) custom-call(bf16[32,2,8,128]{3,2,1,0:T(8,128)(2,1)} %bitcast.8, bf16[27,32,64]{2,1,0:T(8,128)(2,1)} %bitcast.7, bf16[27,64,128]{2,1,0:T(8,128)(2,1)} %bitcast.6, bf16[128,2,8,128]{3,2,1,0:T(8,128)(2,1)} %bitcast.5), custom_call_target="tpu_custom_call" | custom-call | tf_op jit(solution)/shard_map/pallas_call | solution.py:546
  38.7 0.9 %shard_map.68 = (bf16[128,2,8,128]{3,2,1,0:T(8,128)(2,1)}, f32[27,4,32]{2,1,0:T(4,128)}, f32[27,8,64]{2,1,0:T(8,128)}) custom-call(bf16[128,2,8,128]{3,2,1,0:T(8,128)(2,1)S(1)} %get-tuple-element.9.refs_0_, f32[27,4,32]{2,1,0:T(4,128)S(1)} %get-tuple-element.10.refs_1_, f32[27,8,64]{2,1,0:T(8,128)S(1)} %get-tuple-element.11.refs_2_), custom_call_target="tpu_custom_call" | custom-call | tf_op jit(solution)/shard_map/pallas_call | solution.py:627

commit v6 on v5

--- a/solution.py
+++ b/solution.py
@@ -272,7 +272,7 @@
                     H3[d, h, c * 64 : c * 64 + 64] = shifted(hid, 1 - c).astype(BF)
                     D3[d, h, c * 64 : c * 64 + 64] = shifted(delta, c - 1).astype(BF)
 
-        pl.loop(0, 10, unroll=5)(body)
+        pl.loop(0, 10, unroll=10)(body)
 
     def keep(owner, unit, value):
         if unit < 4:

time: 39.7 us -> 38.4 us (0.967)
  Pallas kernels: 38.9 us -> 37.7 us
    pallas_call x1, Pallas kernels: 38.1 us -> 36.8 us  [per_device(): pl.pallas_call(functools.partial(kernel, sizes), out_shape=(jax.ShapeDtyp...]
where the time goes in v6:
time: 38.4 us; the launch traced here: 38.3 us
  Pallas kernels  37.7 us (98%)
  between operations  0.64 us (2%)
    pallas_call x1, Pallas kernels, per_device(): pl.pallas_call(functools.partial(kernel, sizes), out_shape=(jax.ShapeDtyp...  36.8 us
    pallas_call x1, Pallas kernels, per_device(): pl.pallas_call(write_out, out_shape=tuple((jax.ShapeDtypeStruct(x.shape,...  0.86 us

profile of v6, /device:TPU:1, one launch (start us, length us, event | category | flops | bytes accessed | tf_op | source)
XLA Modules:
  0.0 38.3 jit_solution(8363977679158276565)
XLA Ops:
  0.6 36.8 %shard_map.67 = (bf16[128,2,8,128]{3,2,1,0:T(8,128)(2,1)S(1)}, f32[27,4,32]{2,1,0:T(4,128)S(1)}, f32[27,8,64]{2,1,0:T(8,128)S(1)}) custom-call(bf16[32,2,8,128]{3,2,1,0:T(8,128)(2,1)} %bitcast.8, bf16[27,32,64]{2,1,0:T(8,128)(2,1)} %bitcast.7, bf16[27,64,128]{2,1,0:T(8,128)(2,1)} %bitcast.6, bf16[128,2,8,128]{3,2,1,0:T(8,128)(2,1)} %bitcast.5), custom_call_target="tpu_custom_call" | custom-call | tf_op jit(solution)/shard_map/pallas_call | solution.py:546
  37.5 0.9 %shard_map.68 = (bf16[128,2,8,128]{3,2,1,0:T(8,128)(2,1)}, f32[27,4,32]{2,1,0:T(4,128)}, f32[27,8,64]{2,1,0:T(8,128)}) custom-call(bf16[128,2,8,128]{3,2,1,0:T(8,128)(2,1)S(1)} %get-tuple-element.9.refs_0_, f32[27,4,32]{2,1,0:T(4,128)S(1)} %get-tuple-element.10.refs_1_, f32[27,8,64]{2,1,0:T(8,128)S(1)} %get-tuple-element.11.refs_2_), custom_call_target="tpu_custom_call" | custom-call | tf_op jit(solution)/shard_map/pallas_call | solution.py:627

commit v7 on v6

--- a/solution.py
+++ b/solution.py
@@ -253,7 +253,7 @@
 
     def hidden(planes):
         def body(h):
-            ok_h = ((h > 0) | (hgt > 0)) & ((h < 9) | (hgt < n_hgt - 1))
+            ok_h = {0: hgt > 0, 9: hgt < n_hgt - 1}.get(h)
             x = [
                 jnp.concatenate([V[d + a, pl.ds(h, 3)].reshape(96, W) for d in planes], axis=1)
                 for a in range(3)
@@ -263,16 +263,19 @@
                 part = [t[c * 64 : c * 64 + 64, e * W : e * W + W] for c in range(3)]
                 pre = shifted(part[0], 1) + part[1] + shifted(part[2], -1)
                 sigma = 0.5 * jnp.tanh(0.5 * pre) + 0.5
-                ok = {0: ok_h & (dep > 0), 3: ok_h & (dep < n_dep - 1)}.get(d, ok_h)
-                ok = ok.astype(F32)
-                hid = pre * sigma * ok
-                delta = BO[d, h] * (sigma * (1.0 + pre * (1.0 - sigma)) * ok)
+                ok_d = {0: dep > 0, 3: dep < n_dep - 1}.get(d)
+                tests = [test for test in (ok_h, ok_d) if test is not None]
+                hid = pre * sigma
+                delta = BO[d, h] * (sigma * (1.0 + pre * (1.0 - sigma)))
+                for test in tests:
+                    hid, delta = hid * test.astype(F32), delta * test.astype(F32)
                 H[d, h] = hid.astype(BF)
                 for c in range(3):
                     H3[d, h, c * 64 : c * 64 + 64] = shifted(hid, 1 - c).astype(BF)
                     D3[d, h, c * 64 : c * 64 + 64] = shifted(delta, c - 1).astype(BF)
 
-        pl.loop(0, 10, unroll=10)(body)
+        for h in range(10):
+            body(h)
 
     def keep(owner, unit, value):
         if unit < 4:
@@ -429,7 +432,7 @@
     start(ya)
     cb.wait_recv()
 
-    @pl.loop(0, n_z, unroll=4)
+    @pl.loop(0, n_z, unroll=n_z)
     def _(j):
         ZSB[j] = (GB[core, j] + RCB[j].astype(F32)).astype(BF)
 

time: 38.4 us -> 38.5 us (level)
  no operation moved by 1% of the time
where the time goes in v7:
time: 38.5 us; the launch traced here: 38.4 us
  Pallas kernels  37.7 us (98%)
  between operations  0.64 us (2%)
    pallas_call x1, Pallas kernels, per_device(): pl.pallas_call(functools.partial(kernel, sizes), out_shape=(jax.ShapeDtyp...  36.9 us
    pallas_call x1, Pallas kernels, per_device(): pl.pallas_call(write_out, out_shape=tuple((jax.ShapeDtypeStruct(x.shape,...  0.86 us

profile of v7, /device:TPU:1, one launch (start us, length us, event | category | flops | bytes accessed | tf_op | source)
XLA Modules:
  0.0 38.4 jit_solution(6829877035969287769)
XLA Ops:
  0.6 36.9 %shard_map.67 = (bf16[128,2,8,128]{3,2,1,0:T(8,128)(2,1)S(1)}, f32[27,4,32]{2,1,0:T(4,128)S(1)}, f32[27,8,64]{2,1,0:T(8,128)S(1)}) custom-call(bf16[32,2,8,128]{3,2,1,0:T(8,128)(2,1)} %bitcast.8, bf16[27,32,64]{2,1,0:T(8,128)(2,1)} %bitcast.7, bf16[27,64,128]{2,1,0:T(8,128)(2,1)} %bitcast.6, bf16[128,2,8,128]{3,2,1,0:T(8,128)(2,1)} %bitcast.5), custom_call_target="tpu_custom_call" | custom-call | tf_op jit(solution)/shard_map/pallas_call | solution.py:549
  37.5 0.9 %shard_map.68 = (bf16[128,2,8,128]{3,2,1,0:T(8,128)(2,1)}, f32[27,4,32]{2,1,0:T(4,128)}, f32[27,8,64]{2,1,0:T(8,128)}) custom-call(bf16[128,2,8,128]{3,2,1,0:T(8,128)(2,1)S(1)} %get-tuple-element.9.refs_0_, f32[27,4,32]{2,1,0:T(4,128)S(1)} %get-tuple-element.10.refs_1_, f32[27,8,64]{2,1,0:T(8,128)S(1)} %get-tuple-element.11.refs_2_), custom_call_target="tpu_custom_call" | custom-call | tf_op jit(solution)/shard_map/pallas_call | solution.py:630
